TPU v7x, 32 devices: a whole 2x2x4 slice. The times are simulated.
32 devices in a mesh: groups: 2 (over y), pair: 16 (over z, x, core).
Axes of the slice: x: 2, y: 2, z: 4, core: 2. Of those that a mesh axis runs over, the one named last changes fastest.
Arguments:
- layer_inputs: bfloat16 [64, 4, 2304], P(('groups', 'pair')), parts along dimension 0, may hold values from -6 to 6
- encoder: bfloat16 [4, 2304, 16384], P(None, None, 'pair'), may hold values from -0.125 to 0.125
- enc_bias: float32 [4, 16384], P(None, 'pair'), may hold values from -3 to 3
- decoder: bfloat16 [10, 16384, 2304], P(None, 'pair'), may hold values from -0.03125 to 0.03125
- dec_bias: float32 [4, 2304], replicated, may hold values from -3 to 3
- valid_count: int32 [2], P('groups'), parts along dimension 0, may hold values from 16 to 32
Outputs:
- recon: float32 [64, 4, 2304], P(('groups', 'pair')), parts along dimension 0
There are 2 independent parts, one for each index of `groups`. A program takes and returns all parts, laid end to end along the dimension named above; an argument that names none is the same for every part. Nothing has to cross between parts.
Inputs may be any that keep to these rules, and one draw needn't show every extreme that they name: Tokens at rows valid_count[0] and later are padding.
All inputs are finite; a program needn't handle non-finite values.
Results may differ from a plain program's by a relative error of at most 0.0025.
Values may be sent and summed in bfloat16 or wider, within the bound.
No kernel may reach another device: no remote copies, remote signals or barrier semaphores. Data moves between devices by JAX's collectives and lax.ppermute only.
A program may use at most 192 MiB of HBM per device.

v0:
```python
import jax
import jax.numpy as jnp
from jax import lax
from jax.sharding import PartitionSpec as P


def pair_index(source, target, layers):
    return source * layers - source * (source - 1) // 2 + (target - source)


def body(layer_inputs, encoder, enc_bias, decoder, dec_bias, valid_count):
    layers = encoder.shape[0]
    width = layer_inputs.shape[2]
    limit = valid_count[0]
    piece = lax.all_gather(layer_inputs, "pair", axis=0, tiled=True)
    count = piece.shape[0]
    positions = lax.iota(jnp.int32, count)
    keep = (positions < limit)[:, None]
    encoded = []
    for source in range(layers):
        pre = jnp.dot(piece[:, source, :], encoder[source], preferred_element_type=jnp.float32)
        pre = pre + enc_bias[source][None, :]
        encoded.append(jnp.where(keep, jnp.maximum(pre, 0.0), 0.0).astype(jnp.bfloat16))
    feats = jnp.stack(encoded, axis=1)

    def decode_target(chosen, target):
        total = jnp.zeros((chosen.shape[0], width), jnp.float32)
        for source in range(target + 1):
            total = total + jnp.dot(
                chosen[:, source, :],
                decoder[pair_index(source, target, layers)],
                preferred_element_type=jnp.float32,
            )
        return total

    chosen = feats
    summed = lax.psum_scatter(
        jnp.stack([decode_target(chosen, target) for target in range(layers)], axis=1),
        "pair",
        scatter_dimension=0,
        tiled=True,
    )
    return summed + dec_bias[None, :, :]


def solution(mesh):
    return jax.shard_map(
        body,
        mesh=mesh,
        in_specs=(
            P(("groups", "pair"), None, None),
            P(None, None, "pair"),
            P(None, "pair"),
            P(None, "pair", None),
            P(),
            P("groups"),
        ),
        out_specs=P(("groups", "pair"), None, None),
        check_vma=False,
    )
```

profile of v0, /device:TPU:0, one launch (start us, length us, event | category | flops | bytes accessed | tf_op | source)
XLA Modules:
  0.0 179.9 jit_solution(2598196668937922969)
XLA Ops:
  6.5 0.0 all-reduce.3.cloned.1.call-start
  6.5 25.0 %all_gather.3 = bf16[32,4,2304]{2,1,0:T(4,128)(2,1)S(1)} all-gather(bf16[2,4,2304]{2,1,0:T(4,128)(2,1)} %param.6), channel_id=1, replica_groups=mesh['groups'=2,'pair'=16] {'pair'}, dimensions={0}, use_global_device_ids=true | all-gather | bytes 626688 | tf_op jit(solution)/shard_map/all_gather | solution.py:15
  31.6 0.8 fusion.126
  32.4 0.9 fusion.127
  34.0 3.3 %fusion.114 = bf16[32,1024]{1,0:T(8,128)(2,1)S(1)} fusion(bf16[4,2304,1024]{2,1,0:T(8,128)(2,1)} %param.7, bf16[32,1,2304]{2,1,0:T(2,128)(2,1)S(1)} %get-tuple-element.7, f32[1024]{0:T(1024)S(1)} %bitcast.136, pred[32]{0:T(512)(128)(4,1)S(1)} %iota_compare_fusion), kind=kOutput, calls=%fused_computation.67 | convolution fusion | flops 151126016 | bytes 4935712 | tf_op jit(solution)/shard_map/dot_general | solution.py:21
  37.3 3.2 %fusion.6 = f32[32,2304]{1,0:T(8,128)S(1)} fusion(bf16[32,1024]{1,0:T(8,128)(2,1)S(1)} %fusion.114, bf16[10,1024,2304]{2,1,0:T(8,128)(2,1)} %param.9), kind=kOutput, calls=%fused_computation.6 | convolution fusion | flops 150994944 | bytes 5079040 | tf_op jit(solution)/shard_map/dot_general | solution.py:29
  40.5 3.3 %fusion.14 = f32[32,2304]{1,0:T(8,128)S(1)} fusion(bf16[32,1024]{1,0:T(8,128)(2,1)S(1)} %fusion.114, bf16[10,1024,2304]{2,1,0:T(8,128)(2,1)} %param.9), kind=kOutput, calls=%fused_computation.14 | convolution fusion | flops 150994944 | bytes 5079040 | tf_op jit(solution)/shard_map/dot_general | solution.py:29
  43.8 3.3 %fusion.111 = bf16[32,1024]{1,0:T(8,128)(2,1)S(1)} fusion(bf16[4,2304,1024]{2,1,0:T(8,128)(2,1)} %param.7, bf16[32,1,2304]{2,1,0:T(2,128)(2,1)S(1)} %get-tuple-element.6, f32[1024]{0:T(1024)S(1)} %bitcast.135, pred[32]{0:T(512)(128)(4,1)S(1)} %iota_compare_fusion), kind=kOutput, calls=%fused_computation.66 | convolution fusion | flops 151126016 | bytes 4935712 | tf_op jit(solution)/shard_map/dot_general | solution.py:21
  47.0 3.2 %fusion.4 = f32[32,2304]{1,0:T(8,128)S(1)} fusion(bf16[32,1024]{1,0:T(8,128)(2,1)S(1)} %fusion.111, bf16[10,1024,2304]{2,1,0:T(8,128)(2,1)} %param.9), kind=kOutput, calls=%fused_computation.4 | convolution fusion | flops 150994944 | bytes 5079040 | tf_op jit(solution)/shard_map/dot_general | solution.py:29
  50.3 3.3 %fusion.10 = f32[32,2304]{1,0:T(8,128)S(1)} fusion(bf16[32,1024]{1,0:T(8,128)(2,1)S(1)} %fusion.111, bf16[10,1024,2304]{2,1,0:T(8,128)(2,1)} %param.9), kind=kOutput, calls=%fused_computation.10 | convolution fusion | flops 150994944 | bytes 5079040 | tf_op jit(solution)/shard_map/dot_general | solution.py:29
  53.5 3.3 %fusion.18 = f32[32,2304]{1,0:T(8,128)S(1)} fusion(bf16[32,1024]{1,0:T(8,128)(2,1)S(1)} %fusion.114, bf16[10,1024,2304]{2,1,0:T(8,128)(2,1)} %param.9), kind=kOutput, calls=%fused_computation.18 | convolution fusion | flops 150994944 | bytes 5079040 | tf_op jit(solution)/shard_map/dot_general | solution.py:29
  56.8 3.3 %fusion.117 = bf16[32,1024]{1,0:T(8,128)(2,1)S(1)} fusion(bf16[4,2304,1024]{2,1,0:T(8,128)(2,1)} %param.7, bf16[32,1,2304]{2,1,0:T(2,128)(2,1)S(1)} %get-tuple-element.8, f32[1024]{0:T(1024)S(1)} %bitcast.134, pred[32]{0:T(512)(128)(4,1)S(1)} %iota_compare_fusion), kind=kOutput, calls=%fused_computation.68 | convolution fusion | flops 151126016 | bytes 4935712 | tf_op jit(solution)/shard_map/dot_general | solution.py:21
  60.1 3.2 %fusion.69 = f32[32,1,2304]{2,0,1:T(8,128)S(1)} fusion(bf16[32,1024]{1,0:T(8,128)(2,1)S(1)} %fusion.117, bf16[10,1024,2304]{2,1,0:T(8,128)(2,1)} %param.9), kind=kOutput, calls=%fused_computation.51 | convolution fusion | flops 150994944 | bytes 5079040 | tf_op jit(solution)/shard_map/dot_general | solution.py:29
  63.3 3.3 %fusion.66 = f32[32,1,2304]{2,0,1:T(8,128)S(1)} fusion(f32[32,2304]{1,0:T(8,128)S(1)} %fusion.18, bf16[32,1024]{1,0:T(8,128)(2,1)S(1)} %fusion.117, bf16[10,1024,2304]{2,1,0:T(8,128)(2,1)} %param.9), kind=kOutput, calls=%fused_computation.50 | convolution fusion | flops 151068672 | bytes 5373952 | tf_op jit(solution)/shard_map/dot_general | solution.py:29
  66.6 3.3 %fusion.54 = f32[32,2304]{1,0:T(8,128)S(1)} fusion(f32[32,2304]{1,0:T(8,128)S(1)} %fusion.4, f32[32,2304]{1,0:T(8,128)S(1)} %fusion.6, bf16[32,1024]{1,0:T(8,128)(2,1)S(1)} %fusion.117, bf16[10,1024,2304]{2,1,0:T(8,128)(2,1)} %param.9), kind=kOutput, calls=%fused_computation.46 | convolution fusion | flops 151142400 | bytes 5668864 | tf_op jit(solution)/shard_map/dot_general | solution.py:29
  69.8 3.3 %fusion.63 = f32[32,1,2304]{2,0,1:T(8,128)S(1)} fusion(f32[32,2304]{1,0:T(8,128)S(1)} %fusion.10, f32[32,2304]{1,0:T(8,128)S(1)} %fusion.14, bf16[32,1024]{1,0:T(8,128)(2,1)S(1)} %fusion.117, bf16[10,1024,2304]{2,1,0:T(8,128)(2,1)} %param.9), kind=kOutput, calls=%fused_computation.49 | convolution fusion | flops 151142400 | bytes 5668864 | tf_op jit(solution)/shard_map/dot_general | solution.py:29
  73.1 5.4 %fusion.60 = f32[32,1,2304]{2,0,1:T(8,128)S(1)} fusion(f32[32,2304]{1,0:T(8,128)S(1)} %fusion.54, bf16[10,1024,2304]{2,1,0:T(8,128)(2,1)} %param.9, bf16[4,2304,1024]{2,1,0:T(8,128)(2,1)} %param.7, bf16[32,1,2304]{2,1,0:T(2,128)(2,1)S(1)} %get-tuple-element.5, f32[1024]{0:T(1024)S(1)} %bitcast.133, pred[32]{0:T(512)(128)(4,1)S(1)} %iota_compare_fusion), kind=kOutput, calls=%fused_computation.48 | convolution fusion | flops 302194688 | bytes 10178592 | tf_op jit(solution)/shard_map/dot_general | solution.py:29
  78.6 0.0 copy-start
  78.6 0.1 pad_maximum_fusion
  78.7 1.8 copy.14
  80.4 0.0 all-reduce.3.cloned.1.call-update
  80.5 0.6 dynamic-slice
  81.7 89.8 %all-reduce.3.cloned.1.call-done = f32[32,4,2304]{2,1,0:T(4,128)} async-done(((f32[32,4,2304]{2,1,0:T(4,128)}), f32[32,4,2304]{2,1,0:T(4,128)}) %all-reduce.3.cloned.1.call-update) | async-done | bytes 1179664
  171.5 1.5 dynamic-slice_add_fusion
  (4 shorter events, 0.0 us)
Async XLA Ops:
  6.5 164.9 %all-reduce.3.cloned.1.call-start = ((), (), s32[]{:S(2)}) async-start(), calls=%async_computation | async-start | bytes 2359296
  78.6 1.9 %copy-start.1 = (u32[32]{0:T(128)S(1)}, u32[32]{0:T(128)}, u32[]{:S(2)}) copy-start(u32[32]{0:T(128)} %constant.7) | copy-start | bytes 388
  78.6 92.9 %copy-start = (f32[4,2304]{1,0:T(4,128)S(1)}, f32[4,2304]{1,0:T(4,128)}, u32[]{:S(2)}) copy-start(f32[4,2304]{1,0:T(4,128)} %param.10) | copy-start | bytes 110596
Sparse Core Ops, SparseCore 0:
  80.6 90.8 all-reduce.2
where the time goes:
time: 181 us; the launch traced here: 180 us
  waiting for transfers between devices  89.8 us (50%)
  matrix products  44.5 us (25%)
  blocking collectives  25 us (14%)
  between operations  14.8 us (8%)
  local copies, waits for them, and re-layouts  4.12 us (2%)
    unnamed x2, waiting for transfers between devices  89.8 us
    dot_general x10, matrix products, decode_target(): jnp.dot(chosen[:, source, :], decoder[pair_index(source, target, layers)]...  34.7 us
    all_gather x1, blocking collectives, body(): piece = lax.all_gather(layer_inputs, 'pair', axis=0, tiled=True)  25 us
    dot_general x3, matrix products, body(): jnp.dot(piece[:, source, :], encoder[source], preferred_element_type=jnp....  9.81 us
  transfers between devices with their start and end apart: 1, of which 1 were waited for; matrix products, arithmetic and copies ran while one was open for 0% of the time, Pallas kernels for 0%

commit v1 on v0

v1 whole, which is shorter than its diff:
```python
import functools

import jax
import jax.numpy as jnp
from jax import lax
from jax.experimental import pallas as pl
from jax.experimental.pallas import tpu as pltpu
from jax.sharding import PartitionSpec as P

BF16, F32 = jnp.bfloat16, jnp.float32
RING = 3


def pair_index(source, target, layers):
    return source * layers - source * (source - 1) // 2 + (target - source)


def swap(value, mask, size):
    return lax.ppermute(value, "pair", [(i, i ^ mask) for i in range(size)])


def kernel(bits, limit, near, far, encoder, bias, decoder, keep_out, send_out, ring, feats, sems):
    layers, half, _ = near.shape
    rows = 2 * half
    block = rows >> bits
    pairs = [(s, t) for t in range(layers) for s in range(t + 1)]

    def fetch(step):
        source, target = pairs[step]
        return pltpu.make_async_copy(
            decoder.at[pair_index(source, target, layers)], ring.at[step % RING], sems.at[step % RING]
        )

    for step in range(min(RING, len(pairs))):
        fetch(step).start()

    row = lax.broadcasted_iota(jnp.int32, (rows, 1), 0)
    slot = row // block
    owner = jnp.zeros_like(slot)
    for bit in range(bits):
        owner = owner | (((slot >> bit) & 1) << (bits - 1 - bit))
    owner = owner ^ lax.axis_index("pair")
    keep = owner * block + row % block < limit[0]

    for layer in range(layers):
        x = jnp.concatenate([near[layer], far[layer]], axis=0)
        pre = jnp.dot(x, encoder[layer], preferred_element_type=F32) + bias[layer][None, :]
        feats[layer] = jnp.where(keep, jnp.maximum(pre, 0.0), 0.0).astype(BF16)

    total = None
    for step, (source, target) in enumerate(pairs):
        fetch(step).wait()
        part = jnp.dot(feats[source], ring[step % RING], preferred_element_type=F32)
        total = part if source == 0 else total + part
        if step + RING < len(pairs):
            fetch(step + RING).start()
        if source == target:
            keep_out[target] = total[:half]
            send_out[target] = total[half:]


def transcode(bits, limit, near, far, encoder, bias, decoder):
    layers, half, width = near.shape
    features = encoder.shape[2]
    vmem = pl.BlockSpec(memory_space=pltpu.VMEM)
    out = jax.ShapeDtypeStruct((layers, half, width), F32)
    need = RING * features * width * 2 + layers * 2 * half * features * 2
    return pl.pallas_call(
        functools.partial(kernel, bits),
        out_shape=(out, out),
        in_specs=[pl.BlockSpec(memory_space=pltpu.SMEM), vmem, vmem, vmem, vmem, pl.BlockSpec(memory_space=pl.ANY)],
        out_specs=(vmem, vmem),
        scratch_shapes=[
            pltpu.VMEM((RING, features, width), BF16),
            pltpu.VMEM((layers, 2 * half, features), BF16),
            pltpu.SemaphoreType.DMA((RING,)),
        ],
        compiler_params=pltpu.CompilerParams(vmem_limit_bytes=need + (6 << 20)),
        name="transcode",
    )(limit, near, far, pltpu.with_memory_space_constraint(encoder, pltpu.VMEM), bias, decoder)


def body(size, layer_inputs, encoder, enc_bias, decoder, dec_bias, valid_count):
    bits = size.bit_length() - 1
    held = jnp.swapaxes(layer_inputs, 0, 1)
    for bit in reversed(range(1, bits)):
        held = jnp.concatenate([held, swap(held, 1 << bit, size)], axis=1)
    far = swap(held, 1, size)
    total, sent = transcode(bits, valid_count, held, far, encoder, enc_bias, decoder)
    for bit in range(bits):
        wide = bit == 0 or bit == bits - 1
        came = swap(sent if wide else sent.astype(BF16), 1 << bit, size)
        total = total + came.astype(F32)
        count = total.shape[1] // 2
        if bit < bits - 1:
            total, sent = total[:, :count], total[:, count:]
    return jnp.swapaxes(total, 0, 1) + dec_bias[None, :, :]


def solution(mesh):
    return jax.shard_map(
        functools.partial(body, mesh.shape["pair"]),
        mesh=mesh,
        in_specs=(
            P(("groups", "pair"), None, None),
            P(None, None, "pair"),
            P(None, "pair"),
            P(None, "pair", None),
            P(),
            P("groups"),
        ),
        out_specs=P(("groups", "pair"), None, None),
        check_vma=False,
    )
```

time: 181 us -> 60.9 us (0.34)
  waiting for transfers between devices: 89.8 us -> 21.1 us
  matrix products: 44.5 us -> 0 us
  blocking collectives: 25 us -> 0 us
  Pallas kernels: 0 us -> 15.8 us
  between operations: 14.8 us -> 0.72 us
  starting transfers between devices: 0.01 us -> 13.7 us
  local copies, waits for them, and re-layouts: 4.12 us -> 8.64 us
    unnamed x2 -> x0, waiting for transfers between devices: 89.8 us -> none
    dot_general x13 -> x0, matrix products: 44.5 us -> none  [the longest x10 34.7 us: decode_target(): jnp.dot(chosen[:, source, :], decoder[pair_index(source, target, layers)]...]
    all_gather x1 -> x0, blocking collectives: 25 us -> none  [body(): piece = lax.all_gather(layer_inputs, 'pair', axis=0, tiled=True)]
    ppermute x0 -> x8, waiting for transfers between devices: none -> 21.1 us  [swap(): return lax.ppermute(value, 'pair', [(i, i ^ mask) for i in range(size)])]
    pallas_call x0 -> x1, Pallas kernels: none -> 15.8 us  [transcode(): pl.pallas_call(functools.partial(kernel, bits), out_shape=(out, out), in_...]
    ppermute x0 -> x8, starting transfers between devices: none -> 13.7 us  [swap(): return lax.ppermute(value, 'pair', [(i, i ^ mask) for i in range(size)])]
    unnamed x5 -> x7, local copies, waits for them, and re-layouts: 0.59 us -> 7.89 us
  transfers between devices with their start and end apart: 1 -> 8, of which waited for: 1 -> 8; matrix products, arithmetic and copies ran while one was open for 0% -> 0% of each run, Pallas kernels for 0% -> 0%
where the time goes in v1:
time: 60.9 us; the launch traced here: 60.6 us
  waiting for transfers between devices  21.1 us (35%)
  Pallas kernels  15.8 us (26%)
  starting transfers between devices  13.7 us (22%)
  local copies, waits for them, and re-layouts  8.64 us (14%)
  between operations  0.72 us (1%)
    ppermute x8, waiting for transfers between devices, swap(): return lax.ppermute(value, 'pair', [(i, i ^ mask) for i in range(size)])  21.1 us
    pallas_call x1, Pallas kernels, transcode(): pl.pallas_call(functools.partial(kernel, bits), out_shape=(out, out), in_...  15.8 us
    ppermute x8, starting transfers between devices, swap(): return lax.ppermute(value, 'pair', [(i, i ^ mask) for i in range(size)])  13.7 us
    unnamed x7, local copies, waits for them, and re-layouts  7.89 us
  transfers between devices with their start and end apart: 8, of which 8 were waited for; matrix products, arithmetic and copies ran while one was open for 0% of the time, Pallas kernels for 0%

profile of v1, /device:TPU:0, one launch (start us, length us, event | category | flops | bytes accessed | tf_op | source)
XLA Modules:
  0.0 60.6 jit_solution(13972441474265324712)
XLA Ops:
  0.0 0.8 %copy.10 = bf16[2,4,2304]{2,0,1:T(2,128)(2,1)S(1)} copy(bf16[2,4,2304]{2,1,0:T(4,128)(2,1)} %param.6) | data formatting | bytes 73728 | tf_op args[0]
  0.8 4.1 %collective-permute-start = (bf16[4,2,2304]{2,1,0:T(2,128)(2,1)S(1)}, bf16[4,2,2304]{2,1,0:T(2,128)(2,1)S(1)}, u32[]{:S(2)}, u32[]{:S(2)}) collective-permute-start(bf16[4,2,2304]{2,1,0:T(2,128)(2,1)S(1)} %bitcast.5), channel_id=1, source_target_pairs={{0,8},{1,9},{2,10},{3,11},{4,12},{5,13},{6,14},{7,15},{8,0},{9,1},... | collective-permute-start | bytes 110600 | tf_op jit(solution)/shard_map/ppermute | solution.py:19
  4.9 2.3 %collective-permute-done = bf16[4,2,2304]{2,1,0:T(2,128)(2,1)S(1)} collective-permute-done((bf16[4,2,2304]{2,1,0:T(2,128)(2,1)S(1)}, bf16[4,2,2304]{2,1,0:T(2,128)(2,1)S(1)}, u32[]{:S(2)}, u32[]{:S(2)}) %collective-permute-start) | collective-permute-done | bytes 36896 | tf_op jit(solution)/shard_map/ppermute | solution.py:19
  7.2 0.1 pad_maximum_fusion.2
  7.3 1.6 %collective-permute-start.1 = (bf16[4,4,2304]{2,1,0:T(4,128)(2,1)S(1)}, bf16[4,4,2304]{2,1,0:T(4,128)(2,1)S(1)}, u32[]{:S(2)}, u32[]{:S(2)}) collective-permute-start(bf16[4,4,2304]{2,1,0:T(4,128)(2,1)S(1)} %pad_maximum_fusion.2), channel_id=1, source_target_pairs={{0,4},{1,5},{2,6},{3,7},{4,0},{5,1},{6,2},{7,3},{8,12},{9,13},{10,... | collective-permute-start | bytes 221192 | tf_op jit(solution)/shard_map/ppermute | solution.py:19
  8.9 2.8 %collective-permute-done.1 = bf16[4,4,2304]{2,1,0:T(4,128)(2,1)S(1)} collective-permute-done((bf16[4,4,2304]{2,1,0:T(4,128)(2,1)S(1)}, bf16[4,4,2304]{2,1,0:T(4,128)(2,1)S(1)}, u32[]{:S(2)}, u32[]{:S(2)}) %collective-permute-start.1) | collective-permute-done | bytes 73760 | tf_op jit(solution)/shard_map/ppermute | solution.py:19
  11.7 0.1 pad_maximum_fusion.1
  11.9 1.8 %collective-permute-start.2 = (bf16[4,8,2304]{2,1,0:T(8,128)(2,1)S(1)}, bf16[4,8,2304]{2,1,0:T(8,128)(2,1)S(1)}, u32[]{:S(2)}, u32[]{:S(2)}) collective-permute-start(bf16[4,8,2304]{2,1,0:T(8,128)(2,1)S(1)} %pad_maximum_fusion.1), channel_id=1, source_target_pairs={{0,2},{1,3},{2,0},{3,1},{4,6},{5,7},{6,4},{7,5},{8,10},{9,11},{10,... | collective-permute-start | bytes 442376 | tf_op jit(solution)/shard_map/ppermute | solution.py:19
  13.6 3.4 %collective-permute-done.2 = bf16[4,8,2304]{2,1,0:T(8,128)(2,1)S(1)} collective-permute-done((bf16[4,8,2304]{2,1,0:T(8,128)(2,1)S(1)}, bf16[4,8,2304]{2,1,0:T(8,128)(2,1)S(1)}, u32[]{:S(2)}, u32[]{:S(2)}) %collective-permute-start.2) | collective-permute-done | bytes 147488 | tf_op jit(solution)/shard_map/ppermute | solution.py:19
  17.1 0.2 pad_maximum_fusion.near
  17.3 0.1 collective-permute-start.3
  18.0 0.9 %collective-permute-done.3.far = bf16[4,16,2304]{2,1,0:T(8,128)(2,1)S(1)} collective-permute-done((bf16[4,16,2304]{2,1,0:T(8,128)(2,1)S(1)}, bf16[4,16,2304]{2,1,0:T(8,128)(2,1)S(1)}, u32[]{:S(2)}, u32[]{:S(2)}) %collective-permute-start.3) | collective-permute-done | bytes 294944 | tf_op jit(solution)/shard_map/ppermute | solution.py:19
  18.9 6.4 %copy-done = bf16[4,2304,1024]{2,1,0:T(8,128)(2,1)S(1)} copy-done((bf16[4,2304,1024]{2,1,0:T(8,128)(2,1)S(1)}, bf16[4,2304,1024]{2,1,0:T(8,128)(2,1)}, u32[]{:S(2)}) %copy-start) | copy-done | bytes 18874392
  25.3 0.7 %copy-done.1 = f32[4,1024]{1,0:T(4,128)S(1)} copy-done((f32[4,1024]{1,0:T(4,128)S(1)}, f32[4,1024]{1,0:T(4,128)}, u32[]{:S(2)}) %copy-start.1) | copy-done | bytes 16408
  26.0 15.8 %transcode.1 = (f32[4,16,2304]{2,1,0:T(8,128)S(1)}, f32[4,16,2304]{2,1,0:T(8,128)S(1)}) custom-call(s32[1]{0:T(128)S(6)} %copy.11.limit, bf16[4,16,2304]{2,1,0:T(8,128)(2,1)S(1)} %pad_maximum_fusion.near, bf16[4,16,2304]{2,1,0:T(8,128)(2,1)S(1)} %collective-permute-done.3.far, bf16[4,2304,1024]{2,1,0:T(8,128)(2,1)S(1)} %copy-done, f32[4,1024]{1,0:T(4,128)S(1)} %copy-done.1, ...), custom_call_target="tpu_custom_call" | custom-call | tf_op jit(solution)/shard_map/transcode/pallas_call | solution.py:68
  41.8 0.2 collective-permute-start.4
  42.0 1.9 %collective-permute-done.4 = f32[4,16,2304]{2,1,0:T(8,128)S(1)} collective-permute-done((f32[4,16,2304]{2,1,0:T(8,128)S(1)}, f32[4,16,2304]{2,1,0:T(8,128)S(1)}, u32[]{:S(2)}, u32[]{:S(2)}) %collective-permute-start.4) | collective-permute-done | bytes 589856 | tf_op jit(solution)/shard_map/ppermute | solution.py:19
  44.0 1.8 %collective-permute-start.5 = (bf16[4,8,2304]{2,1,0:T(8,128)(2,1)S(1)}, bf16[4,8,2304]{2,1,0:T(8,128)(2,1)S(1)}, u32[]{:S(2)}, u32[]{:S(2)}) collective-permute-start(bf16[4,8,2304]{2,1,0:T(8,128)(2,1)S(1)} %slice.41), channel_id=1, source_target_pairs={{0,2},{1,3},{2,0},{3,1},{4,6},{5,7},{6,4},{7,5},{8,10},{9,11},{10,... | collective-permute-start | bytes 442376 | tf_op jit(solution)/shard_map/ppermute | solution.py:19
  45.8 4.2 %collective-permute-done.5 = bf16[4,8,2304]{2,1,0:T(8,128)(2,1)S(1)} collective-permute-done((bf16[4,8,2304]{2,1,0:T(8,128)(2,1)S(1)}, bf16[4,8,2304]{2,1,0:T(8,128)(2,1)S(1)}, u32[]{:S(2)}, u32[]{:S(2)}) %collective-permute-start.5) | collective-permute-done | bytes 147488 | tf_op jit(solution)/shard_map/ppermute | solution.py:19
  50.0 1.6 %collective-permute-start.6 = (bf16[4,4,2304]{2,1,0:T(4,128)(2,1)S(1)}, bf16[4,4,2304]{2,1,0:T(4,128)(2,1)S(1)}, u32[]{:S(2)}, u32[]{:S(2)}) collective-permute-start(bf16[4,4,2304]{2,1,0:T(4,128)(2,1)S(1)} %slice.42), channel_id=1, source_target_pairs={{0,4},{1,5},{2,6},{3,7},{4,0},{5,1},{6,2},{7,3},{8,12},{9,13},{10,... | collective-permute-start | bytes 221192 | tf_op jit(solution)/shard_map/ppermute | solution.py:19
  51.6 2.8 %collective-permute-done.6 = bf16[4,4,2304]{2,1,0:T(4,128)(2,1)S(1)} collective-permute-done((bf16[4,4,2304]{2,1,0:T(4,128)(2,1)S(1)}, bf16[4,4,2304]{2,1,0:T(4,128)(2,1)S(1)}, u32[]{:S(2)}, u32[]{:S(2)}) %collective-permute-start.6) | collective-permute-done | bytes 73760 | tf_op jit(solution)/shard_map/ppermute | solution.py:19
  54.5 2.6 %collective-permute-start.7 = (f32[4,2,2304]{2,1,0:T(2,128)S(1)}, f32[4,2,2304]{2,1,0:T(2,128)S(1)}, u32[]{:S(2)}, u32[]{:S(2)}) collective-permute-start(f32[4,2,2304]{2,1,0:T(2,128)S(1)} %slice.31), channel_id=1, source_target_pairs={{0,8},{1,9},{2,10},{3,11},{4,12},{5,13},{6,14},{7,15},{8,0},{9,1},... | collective-permute-start | bytes 221192 | tf_op jit(solution)/shard_map/ppermute | solution.py:19
  57.2 2.7 %collective-permute-done.7 = f32[4,2,2304]{2,1,0:T(2,128)S(1)} collective-permute-done((f32[4,2,2304]{2,1,0:T(2,128)S(1)}, f32[4,2,2304]{2,1,0:T(2,128)S(1)}, u32[]{:S(2)}, u32[]{:S(2)}) %collective-permute-start.7) | collective-permute-done | bytes 73760 | tf_op jit(solution)/shard_map/ppermute | solution.py:19
  59.9 0.7 %copy.8 = f32[2,4,2304]{2,1,0:T(4,128)} copy(f32[2,4,2304]{2,0,1:T(2,128)S(1)} %fusion.1) | data formatting | bytes 147456 | tf_op jit(solution)/shard_map/add | solution.py:97
  (11 shorter events, 0.3 us)
Async XLA Ops:
  0.0 59.9 %copy-start.2 = (f32[4,2304]{1,0:T(4,128)S(1)}, f32[4,2304]{1,0:T(4,128)}, u32[]{:S(2)}) copy-start(f32[4,2304]{1,0:T(4,128)} %param.10) | copy-start | bytes 110596
  0.8 6.4 %collective-permute-start = (bf16[4,2,2304]{2,1,0:T(2,128)(2,1)S(1)}, bf16[4,2,2304]{2,1,0:T(2,128)(2,1)S(1)}, u32[]{:S(2)}, u32[]{:S(2)}) collective-permute-start(bf16[4,2,2304]{2,1,0:T(2,128)(2,1)S(1)} %bitcast.5), channel_id=1, source_target_pairs={{0,8},{1,9},{2,10},{3,11},{4,12},{5,13},{6,14},{7,15},{8,0},{9,1},... | collective-permute-start | bytes 110600 | tf_op jit(solution)/shard_map/ppermute | solution.py:19
  7.3 4.4 %collective-permute-start.1 = (bf16[4,4,2304]{2,1,0:T(4,128)(2,1)S(1)}, bf16[4,4,2304]{2,1,0:T(4,128)(2,1)S(1)}, u32[]{:S(2)}, u32[]{:S(2)}) collective-permute-start(bf16[4,4,2304]{2,1,0:T(4,128)(2,1)S(1)} %pad_maximum_fusion.2), channel_id=1, source_target_pairs={{0,4},{1,5},{2,6},{3,7},{4,0},{5,1},{6,2},{7,3},{8,12},{9,13},{10,... | collective-permute-start | bytes 221192 | tf_op jit(solution)/shard_map/ppermute | solution.py:19
  11.9 5.2 %collective-permute-start.2 = (bf16[4,8,2304]{2,1,0:T(8,128)(2,1)S(1)}, bf16[4,8,2304]{2,1,0:T(8,128)(2,1)S(1)}, u32[]{:S(2)}, u32[]{:S(2)}) collective-permute-start(bf16[4,8,2304]{2,1,0:T(8,128)(2,1)S(1)} %pad_maximum_fusion.1), channel_id=1, source_target_pairs={{0,2},{1,3},{2,0},{3,1},{4,6},{5,7},{6,4},{7,5},{8,10},{9,11},{10,... | collective-permute-start | bytes 442376 | tf_op jit(solution)/shard_map/ppermute | solution.py:19
  17.3 1.6 %collective-permute-start.3 = (bf16[4,16,2304]{2,1,0:T(8,128)(2,1)S(1)}, bf16[4,16,2304]{2,1,0:T(8,128)(2,1)S(1)}, u32[]{:S(2)}, u32[]{:S(2)}) collective-permute-start(bf16[4,16,2304]{2,1,0:T(8,128)(2,1)S(1)} %pad_maximum_fusion.near), channel_id=1, source_target_pairs={{0,1},{1,0},{2,3},{3,2},{4,5},{5,4},{6,7},{7,6},{8,9},{9,8},{10,11... | collective-permute-start | bytes 884744 | tf_op jit(solution)/shard_map/ppermute | solution.py:19
  18.9 6.4 %copy-start = (bf16[4,2304,1024]{2,1,0:T(8,128)(2,1)S(1)}, bf16[4,2304,1024]{2,1,0:T(8,128)(2,1)}, u32[]{:S(2)}) copy-start(bf16[4,2304,1024]{2,1,0:T(8,128)(2,1)} %encoder.1) | copy-start | bytes 56623108
  25.3 0.7 %copy-start.1 = (f32[4,1024]{1,0:T(4,128)S(1)}, f32[4,1024]{1,0:T(4,128)}, u32[]{:S(2)}) copy-start(f32[4,1024]{1,0:T(4,128)} %bias.1) | copy-start | bytes 49156
  41.8 2.1 %collective-permute-start.4 = (f32[4,16,2304]{2,1,0:T(8,128)S(1)}, f32[4,16,2304]{2,1,0:T(8,128)S(1)}, u32[]{:S(2)}, u32[]{:S(2)}) collective-permute-start(f32[4,16,2304]{2,1,0:T(8,128)S(1)} %get-tuple-element.8), channel_id=1, source_target_pairs={{0,1},{1,0},{2,3},{3,2},{4,5},{5,4},{6,7},{7,6},{8,9},{9,8},{10,11... | collective-permute-start | bytes 1769480 | tf_op jit(solution)/shard_map/ppermute | solution.py:19
  44.0 6.0 %collective-permute-start.5 = (bf16[4,8,2304]{2,1,0:T(8,128)(2,1)S(1)}, bf16[4,8,2304]{2,1,0:T(8,128)(2,1)S(1)}, u32[]{:S(2)}, u32[]{:S(2)}) collective-permute-start(bf16[4,8,2304]{2,1,0:T(8,128)(2,1)S(1)} %slice.41), channel_id=1, source_target_pairs={{0,2},{1,3},{2,0},{3,1},{4,6},{5,7},{6,4},{7,5},{8,10},{9,11},{10,... | collective-permute-start | bytes 442376 | tf_op jit(solution)/shard_map/ppermute | solution.py:19
  50.0 4.4 %collective-permute-start.6 = (bf16[4,4,2304]{2,1,0:T(4,128)(2,1)S(1)}, bf16[4,4,2304]{2,1,0:T(4,128)(2,1)S(1)}, u32[]{:S(2)}, u32[]{:S(2)}) collective-permute-start(bf16[4,4,2304]{2,1,0:T(4,128)(2,1)S(1)} %slice.42), channel_id=1, source_target_pairs={{0,4},{1,5},{2,6},{3,7},{4,0},{5,1},{6,2},{7,3},{8,12},{9,13},{10,... | collective-permute-start | bytes 221192 | tf_op jit(solution)/shard_map/ppermute | solution.py:19
  54.5 5.3 %collective-permute-start.7 = (f32[4,2,2304]{2,1,0:T(2,128)S(1)}, f32[4,2,2304]{2,1,0:T(2,128)S(1)}, u32[]{:S(2)}, u32[]{:S(2)}) collective-permute-start(f32[4,2,2304]{2,1,0:T(2,128)S(1)} %slice.31), channel_id=1, source_target_pairs={{0,8},{1,9},{2,10},{3,11},{4,12},{5,13},{6,14},{7,15},{8,0},{9,1},... | collective-permute-start | bytes 221192 | tf_op jit(solution)/shard_map/ppermute | solution.py:19

commit v2 on v1

--- a/solution.py
+++ b/solution.py
@@ -19,8 +19,38 @@
     return lax.ppermute(value, "pair", [(i, i ^ mask) for i in range(size)])
 
 
-def kernel(bits, limit, near, far, encoder, bias, decoder, keep_out, send_out, ring, feats, sems):
-    layers, half, _ = near.shape
+def fetch_kernel(spans, after, source, *rest):
+    outs, sems = rest[:-1], rest[-1]
+    copies = [
+        pltpu.make_async_copy(source.at[pl.ds(start, count)], out, sems.at[i])
+        for i, ((start, count), out) in enumerate(zip(spans, outs))
+    ]
+    for copy in copies:
+        copy.start()
+    for copy in copies:
+        copy.wait()
+
+
+def fetch_rows(spans, after, source):
+    any_space = pl.BlockSpec(memory_space=pl.ANY)
+    width = source.shape[1]
+    total = sum(count for _, count in spans) * width * 2
+    return pl.pallas_call(
+        functools.partial(fetch_kernel, spans),
+        out_shape=tuple(jax.ShapeDtypeStruct((count, width), source.dtype) for _, count in spans),
+        in_specs=[any_space, any_space],
+        out_specs=tuple(pl.BlockSpec(memory_space=pltpu.VMEM) for _ in spans),
+        scratch_shapes=[pltpu.SemaphoreType.DMA((len(spans),))],
+        compiler_params=pltpu.CompilerParams(vmem_limit_bytes=1 << 20),
+        cost_estimate=pl.CostEstimate(flops=0, bytes_accessed=2 * total, transcendentals=0),
+        name="fetch_rows",
+    )(after, pltpu.with_memory_space_constraint(source, pltpu.HBM))
+
+
+def kernel(bits, pieces, limit, near, far, bias, decoder, *rest):
+    encoder = rest[: len(pieces)]
+    keep_out, send_out, ring, feats, sems = rest[len(pieces) :]
+    layers, half, width = near.shape
     rows = 2 * half
     block = rows >> bits
     pairs = [(s, t) for t in range(layers) for s in range(t + 1)]
@@ -44,7 +74,12 @@
 
     for layer in range(layers):
         x = jnp.concatenate([near[layer], far[layer]], axis=0)
-        pre = jnp.dot(x, encoder[layer], preferred_element_type=F32) + bias[layer][None, :]
+        pre = bias[layer][None, :]
+        for (start, count), piece in zip(pieces, encoder):
+            first, last = max(start, layer * width), min(start + count, (layer + 1) * width)
+            if first < last:
+                columns = x[:, first - layer * width : last - layer * width]
+                pre = pre + jnp.dot(columns, piece[first - start : last - start], preferred_element_type=F32)
         feats[layer] = jnp.where(keep, jnp.maximum(pre, 0.0), 0.0).astype(BF16)
 
     total = None
@@ -59,16 +94,17 @@
             send_out[target] = total[half:]
 
 
-def transcode(bits, limit, near, far, encoder, bias, decoder):
+def transcode(bits, pieces, limit, near, far, encoder, bias, decoder):
     layers, half, width = near.shape
-    features = encoder.shape[2]
+    features = decoder.shape[1]
     vmem = pl.BlockSpec(memory_space=pltpu.VMEM)
     out = jax.ShapeDtypeStruct((layers, half, width), F32)
     need = RING * features * width * 2 + layers * 2 * half * features * 2
     return pl.pallas_call(
-        functools.partial(kernel, bits),
+        functools.partial(kernel, bits, pieces),
         out_shape=(out, out),
-        in_specs=[pl.BlockSpec(memory_space=pltpu.SMEM), vmem, vmem, vmem, vmem, pl.BlockSpec(memory_space=pl.ANY)],
+        in_specs=[pl.BlockSpec(memory_space=pltpu.SMEM), vmem, vmem, vmem, pl.BlockSpec(memory_space=pl.ANY)]
+        + [vmem] * len(pieces),
         out_specs=(vmem, vmem),
         scratch_shapes=[
             pltpu.VMEM((RING, features, width), BF16),
@@ -77,16 +113,26 @@
         ],
         compiler_params=pltpu.CompilerParams(vmem_limit_bytes=need + (6 << 20)),
         name="transcode",
-    )(limit, near, far, pltpu.with_memory_space_constraint(encoder, pltpu.VMEM), bias, decoder)
+    )(limit, near, far, bias, pltpu.with_memory_space_constraint(decoder, pltpu.HBM), *encoder)
 
 
 def body(size, layer_inputs, encoder, enc_bias, decoder, dec_bias, valid_count):
     bits = size.bit_length() - 1
     held = jnp.swapaxes(layer_inputs, 0, 1)
-    for bit in reversed(range(1, bits)):
-        held = jnp.concatenate([held, swap(held, 1 << bit, size)], axis=1)
+    layers, width = encoder.shape[:2]
+    encoder = encoder.reshape(layers * width, encoder.shape[2])
+    steps = list(reversed(range(1, bits)))
+    cuts = [2 * layers * i // len(steps) * (width // 2) for i in range(len(steps) + 1)]
+    pieces, parts = [], []
+    for i, bit in enumerate(steps):
+        came = swap(held, 1 << bit, size)
+        pieces.append((cuts[i], cuts[i + 1] - cuts[i]))
+        (part,) = fetch_rows(pieces[-1:], held, encoder)
+        came, part = lax.optimization_barrier((came, part))
+        parts.append(part)
+        held = jnp.concatenate([held, came], axis=1)
     far = swap(held, 1, size)
-    total, sent = transcode(bits, valid_count, held, far, encoder, enc_bias, decoder)
+    total, sent = transcode(bits, pieces, valid_count, held, far, parts, enc_bias, decoder)
     for bit in range(bits):
         wide = bit == 0 or bit == bits - 1
         came = swap(sent if wide else sent.astype(BF16), 1 << bit, size)

time: 60.9 us -> 54 us (0.89)
  Pallas kernels: 15.8 us -> 24.1 us
  waiting for transfers between devices: 21.1 us -> 13.3 us
  local copies, waits for them, and re-layouts: 8.64 us -> 1.56 us
    pallas_call x1 -> x4, Pallas kernels: 15.8 us -> 24.1 us  [the longest x1 15.7 us: transcode(): pl.pallas_call(functools.partial(kernel, bits, pieces), out_shape=(out, o...]
    ppermute x8, waiting for transfers between devices: 21.1 us -> 13.3 us  [swap(): return lax.ppermute(value, 'pair', [(i, i ^ mask) for i in range(size)])]
    unnamed x7 -> x5, local copies, waits for them, and re-layouts: 7.89 us -> 0.81 us
  transfers between devices with their start and end apart: 8 -> 8, of which waited for: 8 -> 6; matrix products, arithmetic and copies ran while one was open for 0% -> 0% of each run, Pallas kernels for 0% -> 16%
where the time goes in v2:
time: 54 us; the launch traced here: 53.7 us
  Pallas kernels  24.1 us (45%)
  starting transfers between devices  13.3 us (25%)
  waiting for transfers between devices  13.3 us (25%)
  local copies, waits for them, and re-layouts  1.56 us (3%)
  between operations  0.78 us (1%)
  other arithmetic  0.6 us (1%)
    pallas_call x1, Pallas kernels, transcode(): pl.pallas_call(functools.partial(kernel, bits, pieces), out_shape=(out, o...  15.7 us
    ppermute x8, starting transfers between devices, swap(): return lax.ppermute(value, 'pair', [(i, i ^ mask) for i in range(size)])  13.3 us
    ppermute x8, waiting for transfers between devices, swap(): return lax.ppermute(value, 'pair', [(i, i ^ mask) for i in range(size)])  13.3 us
    pallas_call x3, Pallas kernels, fetch_rows(): pl.pallas_call(functools.partial(fetch_kernel, spans), out_shape=tuple((j...  8.38 us
  transfers between devices with their start and end apart: 8, of which 6 were waited for; matrix products, arithmetic and copies ran while one was open for 0% of the time, Pallas kernels for 16%

profile of v2, /device:TPU:0, one launch (start us, length us, event | category | flops | bytes accessed | tf_op | source)
XLA Modules:
  0.0 53.7 jit_solution(6766697155147546597)
XLA Ops:
  0.0 0.8 %copy.10 = bf16[2,4,2304]{2,0,1:T(2,128)(2,1)S(1)} copy(bf16[2,4,2304]{2,1,0:T(4,128)(2,1)} %param.6) | data formatting | bytes 73728 | tf_op args[0]
  0.8 4.1 %collective-permute-start = (bf16[4,2,2304]{2,1,0:T(2,128)(2,1)S(1)}, bf16[4,2,2304]{2,1,0:T(2,128)(2,1)S(1)}, u32[]{:S(2)}, u32[]{:S(2)}) collective-permute-start(bf16[4,2,2304]{2,1,0:T(2,128)(2,1)S(1)} %bitcast.6), channel_id=1, source_target_pairs={{0,8},{1,9},{2,10},{3,11},{4,12},{5,13},{6,14},{7,15},{8,0},{9,1},... | collective-permute-start | bytes 110600 | tf_op jit(solution)/shard_map/ppermute | solution.py:19
  4.9 2.3 %fetch_rows.3.rest_0_ = bf16[2304,1024]{1,0:T(8,128)(2,1)S(1)} custom-call(bf16[4,2,2304]{2,1,0:T(2,128)(2,1)S(1)} %bitcast.7, bf16[9216,1024]{1,0:T(8,128)(2,1)} %bitcast.11), custom_call_target="tpu_custom_call" | custom-call | bytes 9437184 | tf_op jit(solution)/shard_map/fetch_rows/pallas_call | solution.py:38
  7.3 0.1 pad_maximum_fusion.2.after
  7.4 1.6 %collective-permute-start.1 = (bf16[4,4,2304]{2,1,0:T(4,128)(2,1)S(1)}, bf16[4,4,2304]{2,1,0:T(4,128)(2,1)S(1)}, u32[]{:S(2)}, u32[]{:S(2)}) collective-permute-start(bf16[4,4,2304]{2,1,0:T(4,128)(2,1)S(1)} %pad_maximum_fusion.2.after), channel_id=1, source_target_pairs={{0,4},{1,5},{2,6},{3,7},{4,0},{5,1},{6,2},{7,3},{8,12},{9,13},{10,... | collective-permute-start | bytes 221192 | tf_op jit(solution)/shard_map/ppermute | solution.py:19
  9.0 3.0 %fetch_rows.4.rest_1_ = bf16[3456,1024]{1,0:T(8,128)(2,1)S(1)} custom-call(bf16[4,4,2304]{2,1,0:T(4,128)(2,1)S(1)} %pad_maximum_fusion.2.after, bf16[9216,1024]{1,0:T(8,128)(2,1)} %bitcast.12), custom_call_target="tpu_custom_call" | custom-call | bytes 14155776 | tf_op jit(solution)/shard_map/fetch_rows/pallas_call | solution.py:38
  12.0 0.1 pad_maximum_fusion.1.after
  12.2 1.6 %collective-permute-start.2 = (bf16[4,8,2304]{2,1,0:T(8,128)(2,1)S(1)}, bf16[4,8,2304]{2,1,0:T(8,128)(2,1)S(1)}, u32[]{:S(2)}, u32[]{:S(2)}) collective-permute-start(bf16[4,8,2304]{2,1,0:T(8,128)(2,1)S(1)} %pad_maximum_fusion.1.after), channel_id=1, source_target_pairs={{0,2},{1,3},{2,0},{3,1},{4,6},{5,7},{6,4},{7,5},{8,10},{9,11},{10,... | collective-permute-start | bytes 442376 | tf_op jit(solution)/shard_map/ppermute | solution.py:19
  13.7 3.0 %fetch_rows.5.rest_2_ = bf16[3456,1024]{1,0:T(8,128)(2,1)S(1)} custom-call(bf16[4,8,2304]{2,1,0:T(8,128)(2,1)S(1)} %pad_maximum_fusion.1.after, bf16[9216,1024]{1,0:T(8,128)(2,1)} %bitcast.13), custom_call_target="tpu_custom_call" | custom-call | bytes 14155776 | tf_op jit(solution)/shard_map/fetch_rows/pallas_call | solution.py:38
  16.8 0.6 %collective-permute-done.2 = bf16[4,8,2304]{2,1,0:T(8,128)(2,1)S(1)} collective-permute-done((bf16[4,8,2304]{2,1,0:T(8,128)(2,1)S(1)}, bf16[4,8,2304]{2,1,0:T(8,128)(2,1)S(1)}, u32[]{:S(2)}, u32[]{:S(2)}) %collective-permute-start.2) | collective-permute-done | bytes 147488 | tf_op jit(solution)/shard_map/ppermute | solution.py:19
  17.4 0.2 pad_maximum_fusion.near
  17.6 0.1 collective-permute-start.3
  18.3 0.9 %collective-permute-done.3.far = bf16[4,16,2304]{2,1,0:T(8,128)(2,1)S(1)} collective-permute-done((bf16[4,16,2304]{2,1,0:T(8,128)(2,1)S(1)}, bf16[4,16,2304]{2,1,0:T(8,128)(2,1)S(1)}, u32[]{:S(2)}, u32[]{:S(2)}) %collective-permute-start.3) | collective-permute-done | bytes 294944 | tf_op jit(solution)/shard_map/ppermute | solution.py:19
  19.2 15.7 %transcode.1 = (f32[4,16,2304]{2,1,0:T(8,128)S(1)}, f32[4,16,2304]{2,1,0:T(8,128)S(1)}) custom-call(s32[1]{0:T(128)S(6)} %copy.11.limit, bf16[4,16,2304]{2,1,0:T(8,128)(2,1)S(1)} %pad_maximum_fusion.near, bf16[4,16,2304]{2,1,0:T(8,128)(2,1)S(1)} %collective-permute-done.3.far, f32[4,1024]{1,0:T(4,128)S(1)} %copy-done, bf16[10,1024,2304]{2,1,0:T(8,128)(2,1)} %decoder.1, ...), custom_call_target="tpu_custom_call" | custom-call | tf_op jit(solution)/shard_map/transcode/pallas_call | solution.py:103
  34.9 0.2 collective-permute-start.4
  35.2 1.9 %collective-permute-done.4 = f32[4,16,2304]{2,1,0:T(8,128)S(1)} collective-permute-done((f32[4,16,2304]{2,1,0:T(8,128)S(1)}, f32[4,16,2304]{2,1,0:T(8,128)S(1)}, u32[]{:S(2)}, u32[]{:S(2)}) %collective-permute-start.4) | collective-permute-done | bytes 589856 | tf_op jit(solution)/shard_map/ppermute | solution.py:19
  37.1 1.6 %collective-permute-start.5 = (bf16[4,8,2304]{2,1,0:T(8,128)(2,1)S(1)}, bf16[4,8,2304]{2,1,0:T(8,128)(2,1)S(1)}, u32[]{:S(2)}, u32[]{:S(2)}) collective-permute-start(bf16[4,8,2304]{2,1,0:T(8,128)(2,1)S(1)} %slice.41), channel_id=1, source_target_pairs={{0,2},{1,3},{2,0},{3,1},{4,6},{5,7},{6,4},{7,5},{8,10},{9,11},{10,... | collective-permute-start | bytes 442376 | tf_op jit(solution)/shard_map/ppermute | solution.py:19
  38.7 4.4 %collective-permute-done.5 = bf16[4,8,2304]{2,1,0:T(8,128)(2,1)S(1)} collective-permute-done((bf16[4,8,2304]{2,1,0:T(8,128)(2,1)S(1)}, bf16[4,8,2304]{2,1,0:T(8,128)(2,1)S(1)}, u32[]{:S(2)}, u32[]{:S(2)}) %collective-permute-start.5) | collective-permute-done | bytes 147488 | tf_op jit(solution)/shard_map/ppermute | solution.py:19
  43.1 1.4 %collective-permute-start.6 = (bf16[4,4,2304]{2,1,0:T(4,128)(2,1)S(1)}, bf16[4,4,2304]{2,1,0:T(4,128)(2,1)S(1)}, u32[]{:S(2)}, u32[]{:S(2)}) collective-permute-start(bf16[4,4,2304]{2,1,0:T(4,128)(2,1)S(1)} %slice.42), channel_id=1, source_target_pairs={{0,4},{1,5},{2,6},{3,7},{4,0},{5,1},{6,2},{7,3},{8,12},{9,13},{10,... | collective-permute-start | bytes 221192 | tf_op jit(solution)/shard_map/ppermute | solution.py:19
  44.5 3.0 %collective-permute-done.6 = bf16[4,4,2304]{2,1,0:T(4,128)(2,1)S(1)} collective-permute-done((bf16[4,4,2304]{2,1,0:T(4,128)(2,1)S(1)}, bf16[4,4,2304]{2,1,0:T(4,128)(2,1)S(1)}, u32[]{:S(2)}, u32[]{:S(2)}) %collective-permute-start.6) | collective-permute-done | bytes 73760 | tf_op jit(solution)/shard_map/ppermute | solution.py:19
  47.6 2.8 %collective-permute-start.7 = (f32[4,2,2304]{2,1,0:T(2,128)S(1)}, f32[4,2,2304]{2,1,0:T(2,128)S(1)}, u32[]{:S(2)}, u32[]{:S(2)}) collective-permute-start(f32[4,2,2304]{2,1,0:T(2,128)S(1)} %slice.31), channel_id=1, source_target_pairs={{0,8},{1,9},{2,10},{3,11},{4,12},{5,13},{6,14},{7,15},{8,0},{9,1},... | collective-permute-start | bytes 221192 | tf_op jit(solution)/shard_map/ppermute | solution.py:19
  50.5 2.5 %collective-permute-done.7 = f32[4,2,2304]{2,1,0:T(2,128)S(1)} collective-permute-done((f32[4,2,2304]{2,1,0:T(2,128)S(1)}, f32[4,2,2304]{2,1,0:T(2,128)S(1)}, u32[]{:S(2)}, u32[]{:S(2)}) %collective-permute-start.7) | collective-permute-done | bytes 73760 | tf_op jit(solution)/shard_map/ppermute | solution.py:19
  53.0 0.1 fusion.1
  53.0 0.7 %copy.8 = f32[2,4,2304]{2,1,0:T(4,128)} copy(f32[2,4,2304]{2,0,1:T(2,128)S(1)} %fusion.1) | data formatting | bytes 147456 | tf_op jit(solution)/shard_map/add | solution.py:143
  (12 shorter events, 0.2 us)
Async XLA Ops:
  0.8 6.5 %collective-permute-start = (bf16[4,2,2304]{2,1,0:T(2,128)(2,1)S(1)}, bf16[4,2,2304]{2,1,0:T(2,128)(2,1)S(1)}, u32[]{:S(2)}, u32[]{:S(2)}) collective-permute-start(bf16[4,2,2304]{2,1,0:T(2,128)(2,1)S(1)} %bitcast.6), channel_id=1, source_target_pairs={{0,8},{1,9},{2,10},{3,11},{4,12},{5,13},{6,14},{7,15},{8,0},{9,1},... | collective-permute-start | bytes 110600 | tf_op jit(solution)/shard_map/ppermute | solution.py:19
  7.4 4.7 %collective-permute-start.1 = (bf16[4,4,2304]{2,1,0:T(4,128)(2,1)S(1)}, bf16[4,4,2304]{2,1,0:T(4,128)(2,1)S(1)}, u32[]{:S(2)}, u32[]{:S(2)}) collective-permute-start(bf16[4,4,2304]{2,1,0:T(4,128)(2,1)S(1)} %pad_maximum_fusion.2.after), channel_id=1, source_target_pairs={{0,4},{1,5},{2,6},{3,7},{4,0},{5,1},{6,2},{7,3},{8,12},{9,13},{10,... | collective-permute-start | bytes 221192 | tf_op jit(solution)/shard_map/ppermute | solution.py:19
  12.2 7.1 %copy-start = (f32[4,1024]{1,0:T(4,128)S(1)}, f32[4,1024]{1,0:T(4,128)}, u32[]{:S(2)}) copy-start(f32[4,1024]{1,0:T(4,128)} %bias.1) | copy-start | bytes 49156
  12.2 5.2 %collective-permute-start.2 = (bf16[4,8,2304]{2,1,0:T(8,128)(2,1)S(1)}, bf16[4,8,2304]{2,1,0:T(8,128)(2,1)S(1)}, u32[]{:S(2)}, u32[]{:S(2)}) collective-permute-start(bf16[4,8,2304]{2,1,0:T(8,128)(2,1)S(1)} %pad_maximum_fusion.1.after), channel_id=1, source_target_pairs={{0,2},{1,3},{2,0},{3,1},{4,6},{5,7},{6,4},{7,5},{8,10},{9,11},{10,... | collective-permute-start | bytes 442376 | tf_op jit(solution)/shard_map/ppermute | solution.py:19
  17.6 1.6 %collective-permute-start.3 = (bf16[4,16,2304]{2,1,0:T(8,128)(2,1)S(1)}, bf16[4,16,2304]{2,1,0:T(8,128)(2,1)S(1)}, u32[]{:S(2)}, u32[]{:S(2)}) collective-permute-start(bf16[4,16,2304]{2,1,0:T(8,128)(2,1)S(1)} %pad_maximum_fusion.near), channel_id=1, source_target_pairs={{0,1},{1,0},{2,3},{3,2},{4,5},{5,4},{6,7},{7,6},{8,9},{9,8},{10,11... | collective-permute-start | bytes 884744 | tf_op jit(solution)/shard_map/ppermute | solution.py:19
  18.3 34.7 %copy-start.1 = (f32[4,2304]{1,0:T(4,128)S(1)}, f32[4,2304]{1,0:T(4,128)}, u32[]{:S(2)}) copy-start(f32[4,2304]{1,0:T(4,128)} %param.10) | copy-start | bytes 110596
  34.9 2.1 %collective-permute-start.4 = (f32[4,16,2304]{2,1,0:T(8,128)S(1)}, f32[4,16,2304]{2,1,0:T(8,128)S(1)}, u32[]{:S(2)}, u32[]{:S(2)}) collective-permute-start(f32[4,16,2304]{2,1,0:T(8,128)S(1)} %get-tuple-element.20), channel_id=1, source_target_pairs={{0,1},{1,0},{2,3},{3,2},{4,5},{5,4},{6,7},{7,6},{8,9},{9,8},{10,11... | collective-permute-start | bytes 1769480 | tf_op jit(solution)/shard_map/ppermute | solution.py:19
  37.1 6.0 %collective-permute-start.5 = (bf16[4,8,2304]{2,1,0:T(8,128)(2,1)S(1)}, bf16[4,8,2304]{2,1,0:T(8,128)(2,1)S(1)}, u32[]{:S(2)}, u32[]{:S(2)}) collective-permute-start(bf16[4,8,2304]{2,1,0:T(8,128)(2,1)S(1)} %slice.41), channel_id=1, source_target_pairs={{0,2},{1,3},{2,0},{3,1},{4,6},{5,7},{6,4},{7,5},{8,10},{9,11},{10,... | collective-permute-start | bytes 442376 | tf_op jit(solution)/shard_map/ppermute | solution.py:19
  43.1 4.4 %collective-permute-start.6 = (bf16[4,4,2304]{2,1,0:T(4,128)(2,1)S(1)}, bf16[4,4,2304]{2,1,0:T(4,128)(2,1)S(1)}, u32[]{:S(2)}, u32[]{:S(2)}) collective-permute-start(bf16[4,4,2304]{2,1,0:T(4,128)(2,1)S(1)} %slice.42), channel_id=1, source_target_pairs={{0,4},{1,5},{2,6},{3,7},{4,0},{5,1},{6,2},{7,3},{8,12},{9,13},{10,... | collective-permute-start | bytes 221192 | tf_op jit(solution)/shard_map/ppermute | solution.py:19
  47.6 5.3 %collective-permute-start.7 = (f32[4,2,2304]{2,1,0:T(2,128)S(1)}, f32[4,2,2304]{2,1,0:T(2,128)S(1)}, u32[]{:S(2)}, u32[]{:S(2)}) collective-permute-start(f32[4,2,2304]{2,1,0:T(2,128)S(1)} %slice.31), channel_id=1, source_target_pairs={{0,8},{1,9},{2,10},{3,11},{4,12},{5,13},{6,14},{7,15},{8,0},{9,1},... | collective-permute-start | bytes 221192 | tf_op jit(solution)/shard_map/ppermute | solution.py:19

commit v3 on v1

v3 whole, which is shorter than its diff:
```python
import functools

import jax
import jax.numpy as jnp
from jax import lax
from jax.experimental import pallas as pl
from jax.experimental.pallas import tpu as pltpu
from jax.sharding import PartitionSpec as P

BF16, F32 = jnp.bfloat16, jnp.float32
VMEM = pl.BlockSpec(memory_space=pltpu.VMEM)
SMEM = pl.BlockSpec(memory_space=pltpu.SMEM)
ANY = pl.BlockSpec(memory_space=pl.ANY)
SLOTS = 4


def pair_index(source, target, layers):
    return source * layers - source * (source - 1) // 2 + (target - source)


def in_hbm(value):
    return pltpu.with_memory_space_constraint(value, pltpu.HBM)


def exchange_steps(size):
    masks = [1 << bit for bit in reversed(range(1, size.bit_length() - 1))]
    steps = [(mask, mask) for mask in masks]
    if len(steps) >= 2:
        steps[-2:] = [(masks[-2], masks[-1]), (masks[-1], masks[-2])]
    return steps


def swap(value, masks, size):
    return lax.ppermute(value, "pair", [(i, i ^ masks[i % 2]) for i in range(size)])


def fetch_kernel(indices, *refs):
    count = len(indices)
    sources, outs, sems = refs[1 : 1 + count], refs[1 + count : -1], refs[-1]
    copies = [
        pltpu.make_async_copy(source if index is None else source.at[index], out, sems.at[i])
        for i, (index, source, out) in enumerate(zip(indices, sources, outs))
    ]
    for copy in copies:
        copy.start()
    for copy in copies:
        copy.wait()


def fetch(after, parts, hidden):
    shapes = [jax.ShapeDtypeStruct(a.shape if i is None else a.shape[1:], a.dtype) for a, i in parts]
    return pl.pallas_call(
        functools.partial(fetch_kernel, [index for _, index in parts]),
        out_shape=tuple(shapes),
        in_specs=[ANY] * (1 + len(parts)),
        out_specs=tuple(VMEM for _ in shapes),
        scratch_shapes=[pltpu.SemaphoreType.DMA((len(parts),))],
        compiler_params=pltpu.CompilerParams(vmem_limit_bytes=1 << 20),
        cost_estimate=pl.CostEstimate(flops=0, bytes_accessed=hidden, transcendentals=0),
        name="fetch",
    )(after, *[in_hbm(array) for array, _ in parts])


def join_kernel(first, second, out):
    count = first.shape[0]
    for layer in range(out.shape[0]):
        out[layer, :count] = first[:, layer, :]
        out[layer, count:] = second[:, layer, :]


def join(first, second):
    count, layers, width = first.shape
    return pl.pallas_call(
        join_kernel,
        out_shape=jax.ShapeDtypeStruct((layers, 2 * count, width), first.dtype),
        in_specs=[VMEM, VMEM],
        out_specs=VMEM,
        compiler_params=pltpu.CompilerParams(vmem_limit_bytes=1 << 20),
        name="join",
    )(first, second)


def transcode_kernel(steps, order, ready, limit, near, far, bias, encoder, decoder, *rest):
    fetched = dict(zip(ready, rest))
    keep_out, send_out, ring, feats, sems = rest[len(ready) :]
    layers, half, width = near.shape

    def stream(step):
        source = fetched[step] if step in fetched else decoder.at[pair_index(*order[step], layers)]
        return pltpu.make_async_copy(source, ring.at[step % SLOTS], sems.at[step % SLOTS])

    for i in range(min(2, SLOTS, len(order))):
        stream(i).start()

    block = half >> len(steps)
    place = lax.broadcasted_iota(jnp.int32, (half, 1), 0)
    slot = lax.div(place, block) if block & (block - 1) else place >> (block.bit_length() - 1)
    me = lax.axis_index("pair")

    def positions(owner):
        start = owner
        for bit, (even_mask, odd_mask) in enumerate(steps):
            mask = even_mask + (odd_mask - even_mask) * (start & 1)
            owner = owner ^ (((slot >> bit) & 1) * mask)
        return owner * block + place - slot * block

    keep = jnp.concatenate([positions(me), positions(me ^ 1)], axis=0) < limit[0]

    for layer in range(layers):
        x = jnp.concatenate([near[layer], far[layer]], axis=0)
        pre = jnp.dot(x, encoder[layer], preferred_element_type=F32) + bias[layer][None, :]
        feats[layer] = jnp.where(keep, jnp.maximum(pre, 0.0), 0.0).astype(BF16)
        if 2 <= layer + 1 < min(SLOTS, len(order)):
            stream(layer + 1).start()

    total = None
    for step, (source, target) in enumerate(order):
        stream(step).wait()
        term = jnp.dot(feats[source], ring[step % SLOTS], preferred_element_type=F32)
        total = term if source == 0 else total + term
        if step + SLOTS < len(order):
            stream(step + SLOTS).start()
        if source == target:
            keep_out[target] = total[:half]
            send_out[target] = total[half:]


def transcode(steps, order, ready, limit, near, far, bias, encoder, decoder, fetched):
    layers, half, width = near.shape
    features = decoder.shape[1]
    out = jax.ShapeDtypeStruct((layers, half, width), F32)
    need = SLOTS * features * width * 2 + layers * 2 * half * features * 2 + 16 * half * width
    return pl.pallas_call(
        functools.partial(transcode_kernel, steps, order, ready),
        out_shape=(out, out),
        in_specs=[SMEM, VMEM, VMEM, VMEM, VMEM, ANY] + [VMEM] * len(fetched),
        out_specs=(VMEM, VMEM),
        scratch_shapes=[
            pltpu.VMEM((SLOTS, features, width), BF16),
            pltpu.VMEM((layers, 2 * half, features), BF16),
            pltpu.SemaphoreType.DMA((SLOTS,)),
        ],
        compiler_params=pltpu.CompilerParams(vmem_limit_bytes=need + (5 << 20)),
        name="transcode",
    )(limit, near, far, bias, encoder, in_hbm(decoder), *fetched)


def body(size, layer_inputs, encoder, enc_bias, decoder, dec_bias, valid_count):
    layers, width, features = encoder.shape
    steps = exchange_steps(size)
    order = [(source, target) for target in range(layers) for source in range(target + 1)]
    ready = [len(order) // 2, len(order) // 2 + 2][: len(steps) - 1]
    fetched = []
    held = layer_inputs
    for i, masks in enumerate(steps):
        came = swap(held, masks, size)
        parts = [(held, None)] if i == 0 else []
        hidden = 2 * features * width
        if i < len(ready):
            parts.append((decoder, pair_index(*order[ready[i]], layers)))
        if i == len(steps) - 1:
            parts.append((enc_bias, None))
            hidden = 4 * layers * features * width
        came, *got = lax.optimization_barrier((came, *(fetch(held, parts, hidden) if parts else ())))
        held = join(got.pop(0), came) if i == 0 else jnp.concatenate([held, came], axis=1)
        if i == len(steps) - 1:
            enc_bias = got.pop()
        fetched += got
    far = swap(held, (1, 1), size)
    total, sent = transcode(steps, order, ready, valid_count, held, far, enc_bias, encoder, decoder, fetched)
    total = total + swap(sent, (1, 1), size)
    for i, masks in reversed(list(enumerate(steps))):
        count = total.shape[1] // 2
        total, sent = total[:, :count], total[:, count:]
        total = total + swap(sent if i == 0 else sent.astype(BF16), masks, size).astype(F32)
    return jnp.swapaxes(total, 0, 1) + dec_bias[None, :, :]


def solution(mesh):
    return jax.shard_map(
        functools.partial(body, mesh.shape["pair"]),
        mesh=mesh,
        in_specs=(
            P(("groups", "pair"), None, None),
            P(None, None, "pair"),
            P(None, "pair"),
            P(None, "pair", None),
            P(),
            P("groups"),
        ),
        out_specs=P(("groups", "pair"), None, None),
        check_vma=False,
    )
```

time: 60.9 us -> 52.1 us (0.86)
  local copies, waits for them, and re-layouts: 8.64 us -> 0.78 us
  waiting for transfers between devices: 21.1 us -> 15.6 us
  Pallas kernels: 15.8 us -> 21.2 us
    unnamed x7 -> x12, local copies, waits for them, and re-layouts: 7.89 us -> 0.03 us
    ppermute x8, waiting for transfers between devices: 21.1 us -> 15.6 us  [swap(): lax.ppermute(value, 'pair', [(i, i ^ masks[i % 2]) for i in range(size)])]
    pallas_call x1 -> x5, Pallas kernels: 15.8 us -> 21.2 us  [the longest x1 14.5 us: transcode(): pl.pallas_call(functools.partial(transcode_kernel, steps, order, ready),...]
    ppermute x8, starting transfers between devices: 13.7 us -> 13.1 us  [swap(): lax.ppermute(value, 'pair', [(i, i ^ masks[i % 2]) for i in range(size)])]
  transfers between devices with their start and end apart: 8 -> 8, of which waited for: 8 -> 7; matrix products, arithmetic and copies ran while one was open for 0% -> 0% of each run, Pallas kernels for 0% -> 13%
where the time goes in v3:
time: 52.1 us; the launch traced here: 51.8 us
  Pallas kernels  21.2 us (41%)
  waiting for transfers between devices  15.6 us (30%)
  starting transfers between devices  13.1 us (25%)
  between operations  0.82 us (2%)
  local copies, waits for them, and re-layouts  0.78 us (1%)
    ppermute x8, waiting for transfers between devices, swap(): lax.ppermute(value, 'pair', [(i, i ^ masks[i % 2]) for i in range(size)])  15.6 us
    pallas_call x1, Pallas kernels, transcode(): pl.pallas_call(functools.partial(transcode_kernel, steps, order, ready),...  14.5 us
    ppermute x8, starting transfers between devices, swap(): lax.ppermute(value, 'pair', [(i, i ^ masks[i % 2]) for i in range(size)])  13.1 us
    pallas_call x3, Pallas kernels, fetch(): pl.pallas_call(functools.partial(fetch_kernel, [index for _, index in par...  6.62 us
  transfers between devices with their start and end apart: 8, of which 7 were waited for; matrix products, arithmetic and copies ran while one was open for 0% of the time, Pallas kernels for 13%

profile of v3, /device:TPU:0, one launch (start us, length us, event | category | flops | bytes accessed | tf_op | source)
XLA Modules:
  0.0 51.8 jit_solution(1760648760126631428)
XLA Ops:
  0.0 4.0 %collective-permute-start = (bf16[2,4,2304]{2,1,0:T(4,128)(2,1)}, bf16[2,4,2304]{2,1,0:T(4,128)(2,1)S(1)}, u32[]{:S(2)}, u32[]{:S(2)}) collective-permute-start(bf16[2,4,2304]{2,1,0:T(4,128)(2,1)} %refs_1_.3), channel_id=1, source_target_pairs={{0,8},{1,9},{2,10},{3,11},{4,12},{5,13},{6,14},{7,15},{8,0},{9,1},... | collective-permute-start | bytes 110600 | tf_op jit(solution)/shard_map/ppermute | solution.py:34
  4.0 2.4 %fetch.3 = (bf16[2,4,2304]{2,1,0:T(4,128)(2,1)S(1)}, bf16[1024,2304]{1,0:T(8,128)(2,1)S(1)}) custom-call(bf16[2,4,2304]{2,1,0:T(4,128)(2,1)} %refs_1_.3, bf16[2,4,2304]{2,1,0:T(4,128)(2,1)} %refs_1_.3, bf16[10,1024,2304]{2,1,0:T(8,128)(2,1)} %decoder.1), custom_call_target="tpu_custom_call" | custom-call | bytes 4718592 | tf_op jit(solution)/shard_map/fetch/pallas_call | solution.py:52
  6.4 0.2 collective-permute-done.second
  6.6 0.1 join.1.refs_0_
  6.8 1.6 %collective-permute-start.1 = (bf16[4,4,2304]{2,1,0:T(4,128)(2,1)S(1)}, bf16[4,4,2304]{2,1,0:T(4,128)(2,1)S(1)}, u32[]{:S(2)}, u32[]{:S(2)}) collective-permute-start(bf16[4,4,2304]{2,1,0:T(4,128)(2,1)S(1)} %join.1.refs_0_), channel_id=1, source_target_pairs={{0,4},{1,3},{2,6},{3,1},{4,0},{5,7},{6,2},{7,5},{8,12},{9,11},{10,... | collective-permute-start | bytes 221192 | tf_op jit(solution)/shard_map/ppermute | solution.py:34
  8.3 3.1 %fetch.4.rest_1_ = bf16[1024,2304]{1,0:T(8,128)(2,1)S(1)} custom-call(bf16[4,4,2304]{2,1,0:T(4,128)(2,1)S(1)} %join.1.refs_0_, bf16[10,1024,2304]{2,1,0:T(8,128)(2,1)} %decoder.1), custom_call_target="tpu_custom_call" | custom-call | bytes 4718592 | tf_op jit(solution)/shard_map/fetch/pallas_call | solution.py:52
  11.5 0.1 pad_maximum_fusion.1.refs_0_
  11.5 1.5 %collective-permute-start.2 = (bf16[4,8,2304]{2,1,0:T(8,128)(2,1)S(1)}, bf16[4,8,2304]{2,1,0:T(8,128)(2,1)S(1)}, u32[]{:S(2)}, u32[]{:S(2)}) collective-permute-start(bf16[4,8,2304]{2,1,0:T(8,128)(2,1)S(1)} %pad_maximum_fusion.1.refs_0_), channel_id=1, source_target_pairs={{0,2},{1,5},{2,0},{3,7},{4,6},{5,1},{6,4},{7,3},{8,10},{9,13},{10,... | collective-permute-start | bytes 442376 | tf_op jit(solution)/shard_map/ppermute | solution.py:34
  13.0 1.1 %fetch.5.bias = f32[4,1024]{1,0:T(4,128)S(1)} custom-call(bf16[4,8,2304]{2,1,0:T(8,128)(2,1)S(1)} %pad_maximum_fusion.1.refs_0_, f32[4,1024]{1,0:T(4,128)} %refs_1_.5), custom_call_target="tpu_custom_call" | custom-call | bytes 37748736 | tf_op jit(solution)/shard_map/fetch/pallas_call | solution.py:52
  14.2 2.6 %collective-permute-done.2 = bf16[4,8,2304]{2,1,0:T(8,128)(2,1)S(1)} collective-permute-done((bf16[4,8,2304]{2,1,0:T(8,128)(2,1)S(1)}, bf16[4,8,2304]{2,1,0:T(8,128)(2,1)S(1)}, u32[]{:S(2)}, u32[]{:S(2)}) %collective-permute-start.2) | collective-permute-done | bytes 147488 | tf_op jit(solution)/shard_map/ppermute | solution.py:34
  16.8 0.1 pad_maximum_fusion.near
  16.9 0.1 collective-permute-start.3
  17.6 0.9 %collective-permute-done.3.far = bf16[4,16,2304]{2,1,0:T(8,128)(2,1)S(1)} collective-permute-done((bf16[4,16,2304]{2,1,0:T(8,128)(2,1)S(1)}, bf16[4,16,2304]{2,1,0:T(8,128)(2,1)S(1)}, u32[]{:S(2)}, u32[]{:S(2)}) %collective-permute-start.3) | collective-permute-done | bytes 294944 | tf_op jit(solution)/shard_map/ppermute | solution.py:34
  18.6 14.5 %transcode.1 = (f32[4,16,2304]{2,1,0:T(8,128)S(1)}, f32[4,16,2304]{2,1,0:T(8,128)S(1)}) custom-call(s32[1]{0:T(128)S(6)} %copy.8.limit, bf16[4,16,2304]{2,1,0:T(8,128)(2,1)S(1)} %pad_maximum_fusion.near, bf16[4,16,2304]{2,1,0:T(8,128)(2,1)S(1)} %collective-permute-done.3.far, f32[4,1024]{1,0:T(4,128)S(1)} %fetch.5.bias, bf16[4,2304,1024]{2,1,0:T(8,128)(2,1)S(1)} %bitcast.3, ...), custom_call_target="tpu_custom_call" | custom-call | tf_op jit(solution)/shard_map/transcode/pallas_call | solution.py:133
  33.1 0.2 collective-permute-start.4
  33.2 1.9 %collective-permute-done.4 = f32[4,16,2304]{2,1,0:T(8,128)S(1)} collective-permute-done((f32[4,16,2304]{2,1,0:T(8,128)S(1)}, f32[4,16,2304]{2,1,0:T(8,128)S(1)}, u32[]{:S(2)}, u32[]{:S(2)}) %collective-permute-start.4) | collective-permute-done | bytes 589856 | tf_op jit(solution)/shard_map/ppermute | solution.py:34
  35.2 1.5 %collective-permute-start.5 = (bf16[4,8,2304]{2,1,0:T(8,128)(2,1)S(1)}, bf16[4,8,2304]{2,1,0:T(8,128)(2,1)S(1)}, u32[]{:S(2)}, u32[]{:S(2)}) collective-permute-start(bf16[4,8,2304]{2,1,0:T(8,128)(2,1)S(1)} %slice.41), channel_id=1, source_target_pairs={{0,2},{1,5},{2,0},{3,7},{4,6},{5,1},{6,4},{7,3},{8,10},{9,13},{10,... | collective-permute-start | bytes 442376 | tf_op jit(solution)/shard_map/ppermute | solution.py:34
  36.7 3.7 %collective-permute-done.5 = bf16[4,8,2304]{2,1,0:T(8,128)(2,1)S(1)} collective-permute-done((bf16[4,8,2304]{2,1,0:T(8,128)(2,1)S(1)}, bf16[4,8,2304]{2,1,0:T(8,128)(2,1)S(1)}, u32[]{:S(2)}, u32[]{:S(2)}) %collective-permute-start.5) | collective-permute-done | bytes 147488 | tf_op jit(solution)/shard_map/ppermute | solution.py:34
  40.5 1.3 %collective-permute-start.6 = (bf16[4,4,2304]{2,1,0:T(4,128)(2,1)S(1)}, bf16[4,4,2304]{2,1,0:T(4,128)(2,1)S(1)}, u32[]{:S(2)}, u32[]{:S(2)}) collective-permute-start(bf16[4,4,2304]{2,1,0:T(4,128)(2,1)S(1)} %slice.42), channel_id=1, source_target_pairs={{0,4},{1,3},{2,6},{3,1},{4,0},{5,7},{6,2},{7,5},{8,12},{9,11},{10,... | collective-permute-start | bytes 221192 | tf_op jit(solution)/shard_map/ppermute | solution.py:34
  41.8 3.1 %collective-permute-done.6 = bf16[4,4,2304]{2,1,0:T(4,128)(2,1)S(1)} collective-permute-done((bf16[4,4,2304]{2,1,0:T(4,128)(2,1)S(1)}, bf16[4,4,2304]{2,1,0:T(4,128)(2,1)S(1)}, u32[]{:S(2)}, u32[]{:S(2)}) %collective-permute-start.6) | collective-permute-done | bytes 73760 | tf_op jit(solution)/shard_map/ppermute | solution.py:34
  45.0 2.9 %collective-permute-start.7 = (f32[4,2,2304]{2,1,0:T(2,128)S(1)}, f32[4,2,2304]{2,1,0:T(2,128)S(1)}, u32[]{:S(2)}, u32[]{:S(2)}) collective-permute-start(f32[4,2,2304]{2,1,0:T(2,128)S(1)} %slice.31), channel_id=1, source_target_pairs={{0,8},{1,9},{2,10},{3,11},{4,12},{5,13},{6,14},{7,15},{8,0},{9,1},... | collective-permute-start | bytes 221192 | tf_op jit(solution)/shard_map/ppermute | solution.py:34
  47.9 3.2 %collective-permute-done.7 = f32[4,2,2304]{2,1,0:T(2,128)S(1)} collective-permute-done((f32[4,2,2304]{2,1,0:T(2,128)S(1)}, f32[4,2,2304]{2,1,0:T(2,128)S(1)}, u32[]{:S(2)}, u32[]{:S(2)}) %collective-permute-start.7) | collective-permute-done | bytes 73760 | tf_op jit(solution)/shard_map/ppermute | solution.py:34
  51.1 0.1 fusion.1
  51.2 0.7 %copy.7 = f32[2,4,2304]{2,1,0:T(4,128)} copy(f32[2,4,2304]{2,0,1:T(2,128)S(1)} %fusion.1) | data formatting | bytes 147456 | tf_op jit(solution)/shard_map/add | solution.py:176
  (20 shorter events, 0.3 us)
Async XLA Ops:
  0.0 6.6 %collective-permute-start = (bf16[2,4,2304]{2,1,0:T(4,128)(2,1)}, bf16[2,4,2304]{2,1,0:T(4,128)(2,1)S(1)}, u32[]{:S(2)}, u32[]{:S(2)}) collective-permute-start(bf16[2,4,2304]{2,1,0:T(4,128)(2,1)} %refs_1_.3), channel_id=1, source_target_pairs={{0,8},{1,9},{2,10},{3,11},{4,12},{5,13},{6,14},{7,15},{8,0},{9,1},... | collective-permute-start | bytes 110600 | tf_op jit(solution)/shard_map/ppermute | solution.py:34
  6.6 11.9 %slice-start = ((s8[18874368]{0:T(1024)(128)(4,1)}), s8[4194304]{0:T(1024)(128)(4,1)S(1)}, s32[]{:S(2)}) async-start(s8[18874368]{0:T(1024)(128)(4,1)} %bitcast.2), calls=%async_computation | async-start | bytes 8388608
  6.7 11.8 %slice-start.1 = ((s8[18874368]{0:T(1024)(128)(4,1)}), s8[4194304]{0:T(1024)(128)(4,1)S(1)}, s32[]{:S(2)}) async-start(s8[18874368]{0:T(1024)(128)(4,1)} %bitcast.2), calls=%async_computation.1 | async-start | bytes 8388608
  6.7 11.8 %slice-start.2 = ((s8[18874368]{0:T(1024)(128)(4,1)}), s8[4194304]{0:T(1024)(128)(4,1)S(1)}, s32[]{:S(2)}) async-start(s8[18874368]{0:T(1024)(128)(4,1)} %bitcast.2), calls=%async_computation.2 | async-start | bytes 8388608
  6.7 11.8 %slice-start.3 = ((s8[18874368]{0:T(1024)(128)(4,1)}), s8[4194304]{0:T(1024)(128)(4,1)S(1)}, s32[]{:S(2)}) async-start(s8[18874368]{0:T(1024)(128)(4,1)} %bitcast.2), calls=%async_computation.3 | async-start | bytes 8388608
  6.7 11.8 %slice-start.4 = ((s8[18874368]{0:T(1024)(128)(4,1)}), s8[2097152]{0:T(1024)(128)(4,1)S(1)}, s32[]{:S(2)}) async-start(s8[18874368]{0:T(1024)(128)(4,1)} %bitcast.2), calls=%async_computation.4 | async-start | bytes 4194304
  6.8 4.7 %collective-permute-start.1 = (bf16[4,4,2304]{2,1,0:T(4,128)(2,1)S(1)}, bf16[4,4,2304]{2,1,0:T(4,128)(2,1)S(1)}, u32[]{:S(2)}, u32[]{:S(2)}) collective-permute-start(bf16[4,4,2304]{2,1,0:T(4,128)(2,1)S(1)} %join.1.refs_0_), channel_id=1, source_target_pairs={{0,4},{1,3},{2,6},{3,1},{4,0},{5,7},{6,2},{7,5},{8,12},{9,11},{10,... | collective-permute-start | bytes 221192 | tf_op jit(solution)/shard_map/ppermute | solution.py:34
  11.5 5.2 %collective-permute-start.2 = (bf16[4,8,2304]{2,1,0:T(8,128)(2,1)S(1)}, bf16[4,8,2304]{2,1,0:T(8,128)(2,1)S(1)}, u32[]{:S(2)}, u32[]{:S(2)}) collective-permute-start(bf16[4,8,2304]{2,1,0:T(8,128)(2,1)S(1)} %pad_maximum_fusion.1.refs_0_), channel_id=1, source_target_pairs={{0,2},{1,5},{2,0},{3,7},{4,6},{5,1},{6,4},{7,3},{8,10},{9,13},{10,... | collective-permute-start | bytes 442376 | tf_op jit(solution)/shard_map/ppermute | solution.py:34
  16.9 1.6 %collective-permute-start.3 = (bf16[4,16,2304]{2,1,0:T(8,128)(2,1)S(1)}, bf16[4,16,2304]{2,1,0:T(8,128)(2,1)S(1)}, u32[]{:S(2)}, u32[]{:S(2)}) collective-permute-start(bf16[4,16,2304]{2,1,0:T(8,128)(2,1)S(1)} %pad_maximum_fusion.near), channel_id=1, source_target_pairs={{0,1},{1,0},{2,3},{3,2},{4,5},{5,4},{6,7},{7,6},{8,9},{9,8},{10,11... | collective-permute-start | bytes 884744 | tf_op jit(solution)/shard_map/ppermute | solution.py:34
  17.6 33.5 %copy-start = (f32[4,2304]{1,0:T(4,128)S(1)}, f32[4,2304]{1,0:T(4,128)}, u32[]{:S(2)}) copy-start(f32[4,2304]{1,0:T(4,128)} %param.10) | copy-start | bytes 110596
  33.1 2.1 %collective-permute-start.4 = (f32[4,16,2304]{2,1,0:T(8,128)S(1)}, f32[4,16,2304]{2,1,0:T(8,128)S(1)}, u32[]{:S(2)}, u32[]{:S(2)}) collective-permute-start(f32[4,16,2304]{2,1,0:T(8,128)S(1)} %get-tuple-element.26), channel_id=1, source_target_pairs={{0,1},{1,0},{2,3},{3,2},{4,5},{5,4},{6,7},{7,6},{8,9},{9,8},{10,11... | collective-permute-start | bytes 1769480 | tf_op jit(solution)/shard_map/ppermute | solution.py:34
  35.2 5.2 %collective-permute-start.5 = (bf16[4,8,2304]{2,1,0:T(8,128)(2,1)S(1)}, bf16[4,8,2304]{2,1,0:T(8,128)(2,1)S(1)}, u32[]{:S(2)}, u32[]{:S(2)}) collective-permute-start(bf16[4,8,2304]{2,1,0:T(8,128)(2,1)S(1)} %slice.41), channel_id=1, source_target_pairs={{0,2},{1,5},{2,0},{3,7},{4,6},{5,1},{6,4},{7,3},{8,10},{9,13},{10,... | collective-permute-start | bytes 442376 | tf_op jit(solution)/shard_map/ppermute | solution.py:34
  40.5 4.4 %collective-permute-start.6 = (bf16[4,4,2304]{2,1,0:T(4,128)(2,1)S(1)}, bf16[4,4,2304]{2,1,0:T(4,128)(2,1)S(1)}, u32[]{:S(2)}, u32[]{:S(2)}) collective-permute-start(bf16[4,4,2304]{2,1,0:T(4,128)(2,1)S(1)} %slice.42), channel_id=1, source_target_pairs={{0,4},{1,3},{2,6},{3,1},{4,0},{5,7},{6,2},{7,5},{8,12},{9,11},{10,... | collective-permute-start | bytes 221192 | tf_op jit(solution)/shard_map/ppermute | solution.py:34
  45.0 6.1 %collective-permute-start.7 = (f32[4,2,2304]{2,1,0:T(2,128)S(1)}, f32[4,2,2304]{2,1,0:T(2,128)S(1)}, u32[]{:S(2)}, u32[]{:S(2)}) collective-permute-start(f32[4,2,2304]{2,1,0:T(2,128)S(1)} %slice.31), channel_id=1, source_target_pairs={{0,8},{1,9},{2,10},{3,11},{4,12},{5,13},{6,14},{7,15},{8,0},{9,1},... | collective-permute-start | bytes 221192 | tf_op jit(solution)/shard_map/ppermute | solution.py:34

commit v4 on v3

--- a/solution.py
+++ b/solution.py
@@ -38,7 +38,7 @@
     count = len(indices)
     sources, outs, sems = refs[1 : 1 + count], refs[1 + count : -1], refs[-1]
     copies = [
-        pltpu.make_async_copy(source if index is None else source.at[index], out, sems.at[i])
+        pltpu.make_async_copy(source if index is None else source.at[index, pl.ds(0, out.shape[0])], out, sems.at[i])
         for i, (index, source, out) in enumerate(zip(indices, sources, outs))
     ]
     for copy in copies:
@@ -48,9 +48,12 @@
 
 
 def fetch(after, parts, hidden):
-    shapes = [jax.ShapeDtypeStruct(a.shape if i is None else a.shape[1:], a.dtype) for a, i in parts]
+    shapes = [
+        jax.ShapeDtypeStruct(array.shape if index is None else (*rows, array.shape[2]), array.dtype)
+        for array, index, *rows in parts
+    ]
     return pl.pallas_call(
-        functools.partial(fetch_kernel, [index for _, index in parts]),
+        functools.partial(fetch_kernel, [part[1] for part in parts]),
         out_shape=tuple(shapes),
         in_specs=[ANY] * (1 + len(parts)),
         out_specs=tuple(VMEM for _ in shapes),
@@ -58,7 +61,7 @@
         compiler_params=pltpu.CompilerParams(vmem_limit_bytes=1 << 20),
         cost_estimate=pl.CostEstimate(flops=0, bytes_accessed=hidden, transcendentals=0),
         name="fetch",
-    )(after, *[in_hbm(array) for array, _ in parts])
+    )(after, *[in_hbm(part[0]) for part in parts])
 
 
 def join_kernel(first, second, out):
@@ -85,9 +88,29 @@
     keep_out, send_out, ring, feats, sems = rest[len(ready) :]
     layers, half, width = near.shape
 
-    def stream(step):
-        source = fetched[step] if step in fetched else decoder.at[pair_index(*order[step], layers)]
-        return pltpu.make_async_copy(source, ring.at[step % SLOTS], sems.at[step % SLOTS])
+    class Stream:
+        def __init__(self, step):
+            slot, ahead = step % SLOTS, fetched.get(step)
+            rows = 0 if ahead is None else ahead.shape[0]
+            matrix = decoder.at[pair_index(*order[step], layers)]
+            self.copies = []
+            if rows:
+                self.copies.append(pltpu.make_async_copy(ahead, ring.at[slot, pl.ds(0, rows)], sems.at[1, slot]))
+            if rows < ring.shape[1]:
+                rest_rows = pl.ds(rows, ring.shape[1] - rows)
+                self.copies.append(
+                    pltpu.make_async_copy(matrix.at[rest_rows], ring.at[slot, rest_rows], sems.at[0, slot])
+                )
+
+        def start(self):
+            for copy in self.copies:
+                copy.start()
+
+        def wait(self):
+            for copy in self.copies:
+                copy.wait()
+
+    stream = Stream
 
     for i in range(min(2, SLOTS, len(order))):
         stream(i).start()
@@ -138,7 +161,7 @@
         scratch_shapes=[
             pltpu.VMEM((SLOTS, features, width), BF16),
             pltpu.VMEM((layers, 2 * half, features), BF16),
-            pltpu.SemaphoreType.DMA((SLOTS,)),
+            pltpu.SemaphoreType.DMA((2, SLOTS)),
         ],
         compiler_params=pltpu.CompilerParams(vmem_limit_bytes=need + (5 << 20)),
         name="transcode",
@@ -149,15 +172,16 @@
     layers, width, features = encoder.shape
     steps = exchange_steps(size)
     order = [(source, target) for target in range(layers) for source in range(target + 1)]
-    ready = [len(order) // 2, len(order) // 2 + 2][: len(steps) - 1]
+    early = [(len(order) // 2, features), (len(order) // 2 + 2, features * 5 // 8)]
     fetched = []
     held = layer_inputs
     for i, masks in enumerate(steps):
         came = swap(held, masks, size)
         parts = [(held, None)] if i == 0 else []
         hidden = 2 * features * width
-        if i < len(ready):
-            parts.append((decoder, pair_index(*order[ready[i]], layers)))
+        if i < len(early):
+            step, rows = early[i]
+            parts.append((decoder, pair_index(*order[step], layers), rows))
         if i == len(steps) - 1:
             parts.append((enc_bias, None))
             hidden = 4 * layers * features * width
@@ -167,7 +191,7 @@
             enc_bias = got.pop()
         fetched += got
     far = swap(held, (1, 1), size)
-    total, sent = transcode(steps, order, ready, valid_count, held, far, enc_bias, encoder, decoder, fetched)
+    total, sent = transcode(steps, order, [step for step, _ in early], valid_count, held, far, enc_bias, encoder, decoder, fetched)
     total = total + swap(sent, (1, 1), size)
     for i, masks in reversed(list(enumerate(steps))):
         count = total.shape[1] // 2

time: 52.1 us -> 51 us (0.979)
  waiting for transfers between devices: 15.6 us -> 14.7 us
  Pallas kernels: 21.2 us -> 20.3 us
  starting transfers between devices: 13.1 us -> 13.7 us
    pallas_call x3, Pallas kernels: 6.62 us -> 5.71 us  [fetch(): pl.pallas_call(functools.partial(fetch_kernel, [part[1] for part in parts...]
    ppermute x8, waiting for transfers between devices: 15.6 us -> 14.7 us  [swap(): lax.ppermute(value, 'pair', [(i, i ^ masks[i % 2]) for i in range(size)])]
    ppermute x8, starting transfers between devices: 13.1 us -> 13.7 us  [swap(): lax.ppermute(value, 'pair', [(i, i ^ masks[i % 2]) for i in range(size)])]
  transfers between devices with their start and end apart: 8 -> 8, of which waited for: 7 -> 8; matrix products, arithmetic and copies ran while one was open for 0% -> 0% of each run, Pallas kernels for 13% -> 11%
where the time goes in v4:
time: 51 us; the launch traced here: 50.8 us
  Pallas kernels  20.3 us (40%)
  waiting for transfers between devices  14.7 us (29%)
  starting transfers between devices  13.7 us (27%)
  between operations  0.81 us (2%)
  local copies, waits for them, and re-layouts  0.78 us (2%)
    ppermute x8, waiting for transfers between devices, swap(): lax.ppermute(value, 'pair', [(i, i ^ masks[i % 2]) for i in range(size)])  14.7 us
    pallas_call x1, Pallas kernels, transcode(): pl.pallas_call(functools.partial(transcode_kernel, steps, order, ready),...  14.5 us
    ppermute x8, starting transfers between devices, swap(): lax.ppermute(value, 'pair', [(i, i ^ masks[i % 2]) for i in range(size)])  13.7 us
    pallas_call x3, Pallas kernels, fetch(): pl.pallas_call(functools.partial(fetch_kernel, [part[1] for part in parts...  5.71 us
  transfers between devices with their start and end apart: 8, of which 8 were waited for; matrix products, arithmetic and copies ran while one was open for 0% of the time, Pallas kernels for 11%

profile of v4, /device:TPU:0, one launch (start us, length us, event | category | flops | bytes accessed | tf_op | source)
XLA Modules:
  0.0 50.8 jit_solution(4620274375020791079)
XLA Ops:
  0.0 4.0 %collective-permute-start = (bf16[2,4,2304]{2,1,0:T(4,128)(2,1)}, bf16[2,4,2304]{2,1,0:T(4,128)(2,1)S(1)}, u32[]{:S(2)}, u32[]{:S(2)}) collective-permute-start(bf16[2,4,2304]{2,1,0:T(4,128)(2,1)} %refs_1_.3), channel_id=1, source_target_pairs={{0,8},{1,9},{2,10},{3,11},{4,12},{5,13},{6,14},{7,15},{8,0},{9,1},... | collective-permute-start | bytes 110600 | tf_op jit(solution)/shard_map/ppermute | solution.py:34
  4.0 2.4 %fetch.3 = (bf16[2,4,2304]{2,1,0:T(4,128)(2,1)S(1)}, bf16[1024,2304]{1,0:T(8,128)(2,1)S(1)}) custom-call(bf16[2,4,2304]{2,1,0:T(4,128)(2,1)} %refs_1_.3, bf16[2,4,2304]{2,1,0:T(4,128)(2,1)} %refs_1_.3, bf16[10,1024,2304]{2,1,0:T(8,128)(2,1)} %decoder.1), custom_call_target="tpu_custom_call" | custom-call | bytes 4718592 | tf_op jit(solution)/shard_map/fetch/pallas_call | solution.py:55
  6.4 0.2 collective-permute-done.second
  6.6 0.1 join.1.refs_0_
  6.8 1.6 %collective-permute-start.1 = (bf16[4,4,2304]{2,1,0:T(4,128)(2,1)S(1)}, bf16[4,4,2304]{2,1,0:T(4,128)(2,1)S(1)}, u32[]{:S(2)}, u32[]{:S(2)}) collective-permute-start(bf16[4,4,2304]{2,1,0:T(4,128)(2,1)S(1)} %join.1.refs_0_), channel_id=1, source_target_pairs={{0,4},{1,3},{2,6},{3,1},{4,0},{5,7},{6,2},{7,5},{8,12},{9,11},{10,... | collective-permute-start | bytes 221192 | tf_op jit(solution)/shard_map/ppermute | solution.py:34
  8.3 2.6 %fetch.4.rest_1_ = bf16[640,2304]{1,0:T(8,128)(2,1)S(1)} custom-call(bf16[4,4,2304]{2,1,0:T(4,128)(2,1)S(1)} %join.1.refs_0_, bf16[10,1024,2304]{2,1,0:T(8,128)(2,1)} %decoder.1), custom_call_target="tpu_custom_call" | custom-call | bytes 4718592 | tf_op jit(solution)/shard_map/fetch/pallas_call | solution.py:55
  10.9 0.2 collective-permute-done.1
  11.2 0.1 pad_maximum_fusion.1.refs_0_
  11.2 1.8 %collective-permute-start.2 = (bf16[4,8,2304]{2,1,0:T(8,128)(2,1)S(1)}, bf16[4,8,2304]{2,1,0:T(8,128)(2,1)S(1)}, u32[]{:S(2)}, u32[]{:S(2)}) collective-permute-start(bf16[4,8,2304]{2,1,0:T(8,128)(2,1)S(1)} %pad_maximum_fusion.1.refs_0_), channel_id=1, source_target_pairs={{0,2},{1,5},{2,0},{3,7},{4,6},{5,1},{6,4},{7,3},{8,10},{9,13},{10,... | collective-permute-start | bytes 442376 | tf_op jit(solution)/shard_map/ppermute | solution.py:34
  13.0 0.7 %fetch.5.bias = f32[4,1024]{1,0:T(4,128)S(1)} custom-call(bf16[4,8,2304]{2,1,0:T(8,128)(2,1)S(1)} %pad_maximum_fusion.1.refs_0_, f32[4,1024]{1,0:T(4,128)} %refs_1_.5), custom_call_target="tpu_custom_call" | custom-call | bytes 37748736 | tf_op jit(solution)/shard_map/fetch/pallas_call | solution.py:55
  13.7 2.7 %collective-permute-done.2 = bf16[4,8,2304]{2,1,0:T(8,128)(2,1)S(1)} collective-permute-done((bf16[4,8,2304]{2,1,0:T(8,128)(2,1)S(1)}, bf16[4,8,2304]{2,1,0:T(8,128)(2,1)S(1)}, u32[]{:S(2)}, u32[]{:S(2)}) %collective-permute-start.2) | collective-permute-done | bytes 147488 | tf_op jit(solution)/shard_map/ppermute | solution.py:34
  16.5 0.1 pad_maximum_fusion.near
  16.6 0.1 collective-permute-start.3
  17.3 0.9 %collective-permute-done.3.far = bf16[4,16,2304]{2,1,0:T(8,128)(2,1)S(1)} collective-permute-done((bf16[4,16,2304]{2,1,0:T(8,128)(2,1)S(1)}, bf16[4,16,2304]{2,1,0:T(8,128)(2,1)S(1)}, u32[]{:S(2)}, u32[]{:S(2)}) %collective-permute-start.3) | collective-permute-done | bytes 294944 | tf_op jit(solution)/shard_map/ppermute | solution.py:34
  18.3 14.5 %transcode.1 = (f32[4,16,2304]{2,1,0:T(8,128)S(1)}, f32[4,16,2304]{2,1,0:T(8,128)S(1)}) custom-call(s32[1]{0:T(128)S(6)} %copy.8.limit, bf16[4,16,2304]{2,1,0:T(8,128)(2,1)S(1)} %pad_maximum_fusion.near, bf16[4,16,2304]{2,1,0:T(8,128)(2,1)S(1)} %collective-permute-done.3.far, f32[4,1024]{1,0:T(4,128)S(1)} %fetch.5.bias, bf16[4,2304,1024]{2,1,0:T(8,128)(2,1)S(1)} %bitcast.3, ...), custom_call_target="tpu_custom_call" | custom-call | tf_op jit(solution)/shard_map/transcode/pallas_call | solution.py:156
  32.8 0.2 collective-permute-start.4
  33.0 1.9 %collective-permute-done.4 = f32[4,16,2304]{2,1,0:T(8,128)S(1)} collective-permute-done((f32[4,16,2304]{2,1,0:T(8,128)S(1)}, f32[4,16,2304]{2,1,0:T(8,128)S(1)}, u32[]{:S(2)}, u32[]{:S(2)}) %collective-permute-start.4) | collective-permute-done | bytes 589856 | tf_op jit(solution)/shard_map/ppermute | solution.py:34
  35.0 1.8 %collective-permute-start.5 = (bf16[4,8,2304]{2,1,0:T(8,128)(2,1)S(1)}, bf16[4,8,2304]{2,1,0:T(8,128)(2,1)S(1)}, u32[]{:S(2)}, u32[]{:S(2)}) collective-permute-start(bf16[4,8,2304]{2,1,0:T(8,128)(2,1)S(1)} %slice.41), channel_id=1, source_target_pairs={{0,2},{1,5},{2,0},{3,7},{4,6},{5,1},{6,4},{7,3},{8,10},{9,13},{10,... | collective-permute-start | bytes 442376 | tf_op jit(solution)/shard_map/ppermute | solution.py:34
  36.7 3.4 %collective-permute-done.5 = bf16[4,8,2304]{2,1,0:T(8,128)(2,1)S(1)} collective-permute-done((bf16[4,8,2304]{2,1,0:T(8,128)(2,1)S(1)}, bf16[4,8,2304]{2,1,0:T(8,128)(2,1)S(1)}, u32[]{:S(2)}, u32[]{:S(2)}) %collective-permute-start.5) | collective-permute-done | bytes 147488 | tf_op jit(solution)/shard_map/ppermute | solution.py:34
  40.2 1.6 %collective-permute-start.6 = (bf16[4,4,2304]{2,1,0:T(4,128)(2,1)S(1)}, bf16[4,4,2304]{2,1,0:T(4,128)(2,1)S(1)}, u32[]{:S(2)}, u32[]{:S(2)}) collective-permute-start(bf16[4,4,2304]{2,1,0:T(4,128)(2,1)S(1)} %slice.42), channel_id=1, source_target_pairs={{0,4},{1,3},{2,6},{3,1},{4,0},{5,7},{6,2},{7,5},{8,12},{9,11},{10,... | collective-permute-start | bytes 221192 | tf_op jit(solution)/shard_map/ppermute | solution.py:34
  41.8 2.8 %collective-permute-done.6 = bf16[4,4,2304]{2,1,0:T(4,128)(2,1)S(1)} collective-permute-done((bf16[4,4,2304]{2,1,0:T(4,128)(2,1)S(1)}, bf16[4,4,2304]{2,1,0:T(4,128)(2,1)S(1)}, u32[]{:S(2)}, u32[]{:S(2)}) %collective-permute-start.6) | collective-permute-done | bytes 73760 | tf_op jit(solution)/shard_map/ppermute | solution.py:34
  44.7 2.7 %collective-permute-start.7 = (f32[4,2,2304]{2,1,0:T(2,128)S(1)}, f32[4,2,2304]{2,1,0:T(2,128)S(1)}, u32[]{:S(2)}, u32[]{:S(2)}) collective-permute-start(f32[4,2,2304]{2,1,0:T(2,128)S(1)} %slice.31), channel_id=1, source_target_pairs={{0,8},{1,9},{2,10},{3,11},{4,12},{5,13},{6,14},{7,15},{8,0},{9,1},... | collective-permute-start | bytes 221192 | tf_op jit(solution)/shard_map/ppermute | solution.py:34
  47.5 2.6 %collective-permute-done.7 = f32[4,2,2304]{2,1,0:T(2,128)S(1)} collective-permute-done((f32[4,2,2304]{2,1,0:T(2,128)S(1)}, f32[4,2,2304]{2,1,0:T(2,128)S(1)}, u32[]{:S(2)}, u32[]{:S(2)}) %collective-permute-start.7) | collective-permute-done | bytes 73760 | tf_op jit(solution)/shard_map/ppermute | solution.py:34
  50.1 0.7 %copy.7 = f32[2,4,2304]{2,1,0:T(4,128)} copy(f32[2,4,2304]{2,0,1:T(2,128)S(1)} %fusion.1) | data formatting | bytes 147456 | tf_op jit(solution)/shard_map/add | solution.py:200
  (20 shorter events, 0.3 us)
Async XLA Ops:
  0.0 6.6 %collective-permute-start = (bf16[2,4,2304]{2,1,0:T(4,128)(2,1)}, bf16[2,4,2304]{2,1,0:T(4,128)(2,1)S(1)}, u32[]{:S(2)}, u32[]{:S(2)}) collective-permute-start(bf16[2,4,2304]{2,1,0:T(4,128)(2,1)} %refs_1_.3), channel_id=1, source_target_pairs={{0,8},{1,9},{2,10},{3,11},{4,12},{5,13},{6,14},{7,15},{8,0},{9,1},... | collective-permute-start | bytes 110600 | tf_op jit(solution)/shard_map/ppermute | solution.py:34
  6.6 11.7 %slice-start = ((s8[18874368]{0:T(1024)(128)(4,1)}), s8[4194304]{0:T(1024)(128)(4,1)S(1)}, s32[]{:S(2)}) async-start(s8[18874368]{0:T(1024)(128)(4,1)} %bitcast.2), calls=%async_computation | async-start | bytes 8388608
  6.7 11.5 %slice-start.1 = ((s8[18874368]{0:T(1024)(128)(4,1)}), s8[4194304]{0:T(1024)(128)(4,1)S(1)}, s32[]{:S(2)}) async-start(s8[18874368]{0:T(1024)(128)(4,1)} %bitcast.2), calls=%async_computation.1 | async-start | bytes 8388608
  6.7 11.5 %slice-start.2 = ((s8[18874368]{0:T(1024)(128)(4,1)}), s8[4194304]{0:T(1024)(128)(4,1)S(1)}, s32[]{:S(2)}) async-start(s8[18874368]{0:T(1024)(128)(4,1)} %bitcast.2), calls=%async_computation.2 | async-start | bytes 8388608
  6.7 11.5 %slice-start.3 = ((s8[18874368]{0:T(1024)(128)(4,1)}), s8[4194304]{0:T(1024)(128)(4,1)S(1)}, s32[]{:S(2)}) async-start(s8[18874368]{0:T(1024)(128)(4,1)} %bitcast.2), calls=%async_computation.3 | async-start | bytes 8388608
  6.7 11.5 %slice-start.4 = ((s8[18874368]{0:T(1024)(128)(4,1)}), s8[2097152]{0:T(1024)(128)(4,1)S(1)}, s32[]{:S(2)}) async-start(s8[18874368]{0:T(1024)(128)(4,1)} %bitcast.2), calls=%async_computation.4 | async-start | bytes 4194304
  6.8 4.4 %collective-permute-start.1 = (bf16[4,4,2304]{2,1,0:T(4,128)(2,1)S(1)}, bf16[4,4,2304]{2,1,0:T(4,128)(2,1)S(1)}, u32[]{:S(2)}, u32[]{:S(2)}) collective-permute-start(bf16[4,4,2304]{2,1,0:T(4,128)(2,1)S(1)} %join.1.refs_0_), channel_id=1, source_target_pairs={{0,4},{1,3},{2,6},{3,1},{4,0},{5,7},{6,2},{7,5},{8,12},{9,11},{10,... | collective-permute-start | bytes 221192 | tf_op jit(solution)/shard_map/ppermute | solution.py:34
  11.2 5.2 %collective-permute-start.2 = (bf16[4,8,2304]{2,1,0:T(8,128)(2,1)S(1)}, bf16[4,8,2304]{2,1,0:T(8,128)(2,1)S(1)}, u32[]{:S(2)}, u32[]{:S(2)}) collective-permute-start(bf16[4,8,2304]{2,1,0:T(8,128)(2,1)S(1)} %pad_maximum_fusion.1.refs_0_), channel_id=1, source_target_pairs={{0,2},{1,5},{2,0},{3,7},{4,6},{5,1},{6,4},{7,3},{8,10},{9,13},{10,... | collective-permute-start | bytes 442376 | tf_op jit(solution)/shard_map/ppermute | solution.py:34
  16.6 1.6 %collective-permute-start.3 = (bf16[4,16,2304]{2,1,0:T(8,128)(2,1)S(1)}, bf16[4,16,2304]{2,1,0:T(8,128)(2,1)S(1)}, u32[]{:S(2)}, u32[]{:S(2)}) collective-permute-start(bf16[4,16,2304]{2,1,0:T(8,128)(2,1)S(1)} %pad_maximum_fusion.near), channel_id=1, source_target_pairs={{0,1},{1,0},{2,3},{3,2},{4,5},{5,4},{6,7},{7,6},{8,9},{9,8},{10,11... | collective-permute-start | bytes 884744 | tf_op jit(solution)/shard_map/ppermute | solution.py:34
  17.3 32.8 %copy-start = (f32[4,2304]{1,0:T(4,128)S(1)}, f32[4,2304]{1,0:T(4,128)}, u32[]{:S(2)}) copy-start(f32[4,2304]{1,0:T(4,128)} %param.10) | copy-start | bytes 110596
  32.8 2.1 %collective-permute-start.4 = (f32[4,16,2304]{2,1,0:T(8,128)S(1)}, f32[4,16,2304]{2,1,0:T(8,128)S(1)}, u32[]{:S(2)}, u32[]{:S(2)}) collective-permute-start(f32[4,16,2304]{2,1,0:T(8,128)S(1)} %get-tuple-element.26), channel_id=1, source_target_pairs={{0,1},{1,0},{2,3},{3,2},{4,5},{5,4},{6,7},{7,6},{8,9},{9,8},{10,11... | collective-permute-start | bytes 1769480 | tf_op jit(solution)/shard_map/ppermute | solution.py:34
  35.0 5.2 %collective-permute-start.5 = (bf16[4,8,2304]{2,1,0:T(8,128)(2,1)S(1)}, bf16[4,8,2304]{2,1,0:T(8,128)(2,1)S(1)}, u32[]{:S(2)}, u32[]{:S(2)}) collective-permute-start(bf16[4,8,2304]{2,1,0:T(8,128)(2,1)S(1)} %slice.41), channel_id=1, source_target_pairs={{0,2},{1,5},{2,0},{3,7},{4,6},{5,1},{6,4},{7,3},{8,10},{9,13},{10,... | collective-permute-start | bytes 442376 | tf_op jit(solution)/shard_map/ppermute | solution.py:34
  40.2 4.4 %collective-permute-start.6 = (bf16[4,4,2304]{2,1,0:T(4,128)(2,1)S(1)}, bf16[4,4,2304]{2,1,0:T(4,128)(2,1)S(1)}, u32[]{:S(2)}, u32[]{:S(2)}) collective-permute-start(bf16[4,4,2304]{2,1,0:T(4,128)(2,1)S(1)} %slice.42), channel_id=1, source_target_pairs={{0,4},{1,3},{2,6},{3,1},{4,0},{5,7},{6,2},{7,5},{8,12},{9,11},{10,... | collective-permute-start | bytes 221192 | tf_op jit(solution)/shard_map/ppermute | solution.py:34
  44.7 5.3 %collective-permute-start.7 = (f32[4,2,2304]{2,1,0:T(2,128)S(1)}, f32[4,2,2304]{2,1,0:T(2,128)S(1)}, u32[]{:S(2)}, u32[]{:S(2)}) collective-permute-start(f32[4,2,2304]{2,1,0:T(2,128)S(1)} %slice.31), channel_id=1, source_target_pairs={{0,8},{1,9},{2,10},{3,11},{4,12},{5,13},{6,14},{7,15},{8,0},{9,1},... | collective-permute-start | bytes 221192 | tf_op jit(solution)/shard_map/ppermute | solution.py:34

commit v5 on v4

--- a/solution.py
+++ b/solution.py
@@ -12,6 +12,7 @@
 SMEM = pl.BlockSpec(memory_space=pltpu.SMEM)
 ANY = pl.BlockSpec(memory_space=pl.ANY)
 SLOTS = 4
+CHUNK = 768
 
 
 def pair_index(source, target, layers):
@@ -83,10 +84,15 @@
     )(first, second)
 
 
+def chunks(width):
+    return [(start, min(CHUNK, width - start)) for start in range(0, width, CHUNK)]
+
+
 def transcode_kernel(steps, order, ready, limit, near, far, bias, encoder, decoder, *rest):
     fetched = dict(zip(ready, rest))
     keep_out, send_out, ring, feats, sems = rest[len(ready) :]
     layers, half, width = near.shape
+    features = feats.shape[2]
 
     class Stream:
         def __init__(self, step):
@@ -131,15 +137,21 @@
 
     for layer in range(layers):
         x = jnp.concatenate([near[layer], far[layer]], axis=0)
-        pre = jnp.dot(x, encoder[layer], preferred_element_type=F32) + bias[layer][None, :]
-        feats[layer] = jnp.where(keep, jnp.maximum(pre, 0.0), 0.0).astype(BF16)
+        for start, count in chunks(features):
+            columns = pl.ds(start, count)
+            pre = jnp.dot(x, encoder[layer, :, columns], preferred_element_type=F32) + bias[pl.ds(layer, 1), columns]
+            feats[layer, :, columns] = jnp.where(keep, jnp.maximum(pre, 0.0), 0.0).astype(BF16)
         if 2 <= layer + 1 < min(SLOTS, len(order)):
             stream(layer + 1).start()
 
     total = None
     for step, (source, target) in enumerate(order):
         stream(step).wait()
-        term = jnp.dot(feats[source], ring[step % SLOTS], preferred_element_type=F32)
+        terms = [
+            jnp.dot(feats[source], ring[step % SLOTS, :, pl.ds(start, count)], preferred_element_type=F32)
+            for start, count in chunks(width)
+        ]
+        term = jnp.concatenate(terms, axis=1)
         total = term if source == 0 else total + term
         if step + SLOTS < len(order):
             stream(step + SLOTS).start()
@@ -163,7 +175,7 @@
             pltpu.VMEM((layers, 2 * half, features), BF16),
             pltpu.SemaphoreType.DMA((2, SLOTS)),
         ],
-        compiler_params=pltpu.CompilerParams(vmem_limit_bytes=need + (5 << 20)),
+        compiler_params=pltpu.CompilerParams(vmem_limit_bytes=need + (3 << 20)),
         name="transcode",
     )(limit, near, far, bias, encoder, in_hbm(decoder), *fetched)
 

time: 51 us -> 50.4 us (0.988)
    pallas_call x1, Pallas kernels: 14.5 us -> 13.9 us  [transcode(): pl.pallas_call(functools.partial(transcode_kernel, steps, order, ready),...]
where the time goes in v5:
time: 50.4 us; the launch traced here: 50.2 us
  Pallas kernels  19.8 us (39%)
  waiting for transfers between devices  14.7 us (29%)
  starting transfers between devices  13.7 us (27%)
  between operations  0.81 us (2%)
  local copies, waits for them, and re-layouts  0.78 us (2%)
    ppermute x8, waiting for transfers between devices, swap(): lax.ppermute(value, 'pair', [(i, i ^ masks[i % 2]) for i in range(size)])  14.7 us
    pallas_call x1, Pallas kernels, transcode(): pl.pallas_call(functools.partial(transcode_kernel, steps, order, ready),...  13.9 us
    ppermute x8, starting transfers between devices, swap(): lax.ppermute(value, 'pair', [(i, i ^ masks[i % 2]) for i in range(size)])  13.7 us
    pallas_call x3, Pallas kernels, fetch(): pl.pallas_call(functools.partial(fetch_kernel, [part[1] for part in parts...  5.71 us
  transfers between devices with their start and end apart: 8, of which 8 were waited for; matrix products, arithmetic and copies ran while one was open for 0% of the time, Pallas kernels for 11%

profile of v5, /device:TPU:0, one launch (start us, length us, event | category | flops | bytes accessed | tf_op | source)
XLA Modules:
  0.0 50.2 jit_solution(18333487298908746638)
XLA Ops:
  0.0 4.0 %collective-permute-start = (bf16[2,4,2304]{2,1,0:T(4,128)(2,1)}, bf16[2,4,2304]{2,1,0:T(4,128)(2,1)S(1)}, u32[]{:S(2)}, u32[]{:S(2)}) collective-permute-start(bf16[2,4,2304]{2,1,0:T(4,128)(2,1)} %refs_1_.3), channel_id=1, source_target_pairs={{0,8},{1,9},{2,10},{3,11},{4,12},{5,13},{6,14},{7,15},{8,0},{9,1},... | collective-permute-start | bytes 110600 | tf_op jit(solution)/shard_map/ppermute | solution.py:35
  4.0 2.4 %fetch.3 = (bf16[2,4,2304]{2,1,0:T(4,128)(2,1)S(1)}, bf16[1024,2304]{1,0:T(8,128)(2,1)S(1)}) custom-call(bf16[2,4,2304]{2,1,0:T(4,128)(2,1)} %refs_1_.3, bf16[2,4,2304]{2,1,0:T(4,128)(2,1)} %refs_1_.3, bf16[10,1024,2304]{2,1,0:T(8,128)(2,1)} %decoder.1), custom_call_target="tpu_custom_call" | custom-call | bytes 4718592 | tf_op jit(solution)/shard_map/fetch/pallas_call | solution.py:56
  6.4 0.2 collective-permute-done.second
  6.6 0.1 join.1.refs_0_
  6.8 1.6 %collective-permute-start.1 = (bf16[4,4,2304]{2,1,0:T(4,128)(2,1)S(1)}, bf16[4,4,2304]{2,1,0:T(4,128)(2,1)S(1)}, u32[]{:S(2)}, u32[]{:S(2)}) collective-permute-start(bf16[4,4,2304]{2,1,0:T(4,128)(2,1)S(1)} %join.1.refs_0_), channel_id=1, source_target_pairs={{0,4},{1,3},{2,6},{3,1},{4,0},{5,7},{6,2},{7,5},{8,12},{9,11},{10,... | collective-permute-start | bytes 221192 | tf_op jit(solution)/shard_map/ppermute | solution.py:35
  8.3 2.6 %fetch.4.rest_1_ = bf16[640,2304]{1,0:T(8,128)(2,1)S(1)} custom-call(bf16[4,4,2304]{2,1,0:T(4,128)(2,1)S(1)} %join.1.refs_0_, bf16[10,1024,2304]{2,1,0:T(8,128)(2,1)} %decoder.1), custom_call_target="tpu_custom_call" | custom-call | bytes 4718592 | tf_op jit(solution)/shard_map/fetch/pallas_call | solution.py:56
  10.9 0.2 collective-permute-done.1
  11.2 0.1 pad_maximum_fusion.1.refs_0_
  11.2 1.8 %collective-permute-start.2 = (bf16[4,8,2304]{2,1,0:T(8,128)(2,1)S(1)}, bf16[4,8,2304]{2,1,0:T(8,128)(2,1)S(1)}, u32[]{:S(2)}, u32[]{:S(2)}) collective-permute-start(bf16[4,8,2304]{2,1,0:T(8,128)(2,1)S(1)} %pad_maximum_fusion.1.refs_0_), channel_id=1, source_target_pairs={{0,2},{1,5},{2,0},{3,7},{4,6},{5,1},{6,4},{7,3},{8,10},{9,13},{10,... | collective-permute-start | bytes 442376 | tf_op jit(solution)/shard_map/ppermute | solution.py:35
  13.0 0.7 %fetch.5.bias = f32[4,1024]{1,0:T(4,128)S(1)} custom-call(bf16[4,8,2304]{2,1,0:T(8,128)(2,1)S(1)} %pad_maximum_fusion.1.refs_0_, f32[4,1024]{1,0:T(4,128)} %refs_1_.5), custom_call_target="tpu_custom_call" | custom-call | bytes 37748736 | tf_op jit(solution)/shard_map/fetch/pallas_call | solution.py:56
  13.7 2.7 %collective-permute-done.2 = bf16[4,8,2304]{2,1,0:T(8,128)(2,1)S(1)} collective-permute-done((bf16[4,8,2304]{2,1,0:T(8,128)(2,1)S(1)}, bf16[4,8,2304]{2,1,0:T(8,128)(2,1)S(1)}, u32[]{:S(2)}, u32[]{:S(2)}) %collective-permute-start.2) | collective-permute-done | bytes 147488 | tf_op jit(solution)/shard_map/ppermute | solution.py:35
  16.5 0.1 pad_maximum_fusion.near
  16.6 0.1 collective-permute-start.3
  17.3 0.9 %collective-permute-done.3.far = bf16[4,16,2304]{2,1,0:T(8,128)(2,1)S(1)} collective-permute-done((bf16[4,16,2304]{2,1,0:T(8,128)(2,1)S(1)}, bf16[4,16,2304]{2,1,0:T(8,128)(2,1)S(1)}, u32[]{:S(2)}, u32[]{:S(2)}) %collective-permute-start.3) | collective-permute-done | bytes 294944 | tf_op jit(solution)/shard_map/ppermute | solution.py:35
  18.3 13.9 %transcode.1 = (f32[4,16,2304]{2,1,0:T(8,128)S(1)}, f32[4,16,2304]{2,1,0:T(8,128)S(1)}) custom-call(s32[1]{0:T(128)S(6)} %copy.8.limit, bf16[4,16,2304]{2,1,0:T(8,128)(2,1)S(1)} %pad_maximum_fusion.near, bf16[4,16,2304]{2,1,0:T(8,128)(2,1)S(1)} %collective-permute-done.3.far, f32[4,1024]{1,0:T(4,128)S(1)} %fetch.5.bias, bf16[4,2304,1024]{2,1,0:T(8,128)(2,1)S(1)} %bitcast.3, ...), custom_call_target="tpu_custom_call" | custom-call | tf_op jit(solution)/shard_map/transcode/pallas_call | solution.py:168
  32.2 0.2 collective-permute-start.4
  32.4 1.9 %collective-permute-done.4 = f32[4,16,2304]{2,1,0:T(8,128)S(1)} collective-permute-done((f32[4,16,2304]{2,1,0:T(8,128)S(1)}, f32[4,16,2304]{2,1,0:T(8,128)S(1)}, u32[]{:S(2)}, u32[]{:S(2)}) %collective-permute-start.4) | collective-permute-done | bytes 589856 | tf_op jit(solution)/shard_map/ppermute | solution.py:35
  34.4 1.8 %collective-permute-start.5 = (bf16[4,8,2304]{2,1,0:T(8,128)(2,1)S(1)}, bf16[4,8,2304]{2,1,0:T(8,128)(2,1)S(1)}, u32[]{:S(2)}, u32[]{:S(2)}) collective-permute-start(bf16[4,8,2304]{2,1,0:T(8,128)(2,1)S(1)} %slice.41), channel_id=1, source_target_pairs={{0,2},{1,5},{2,0},{3,7},{4,6},{5,1},{6,4},{7,3},{8,10},{9,13},{10,... | collective-permute-start | bytes 442376 | tf_op jit(solution)/shard_map/ppermute | solution.py:35
  36.1 3.4 %collective-permute-done.5 = bf16[4,8,2304]{2,1,0:T(8,128)(2,1)S(1)} collective-permute-done((bf16[4,8,2304]{2,1,0:T(8,128)(2,1)S(1)}, bf16[4,8,2304]{2,1,0:T(8,128)(2,1)S(1)}, u32[]{:S(2)}, u32[]{:S(2)}) %collective-permute-start.5) | collective-permute-done | bytes 147488 | tf_op jit(solution)/shard_map/ppermute | solution.py:35
  39.6 1.6 %collective-permute-start.6 = (bf16[4,4,2304]{2,1,0:T(4,128)(2,1)S(1)}, bf16[4,4,2304]{2,1,0:T(4,128)(2,1)S(1)}, u32[]{:S(2)}, u32[]{:S(2)}) collective-permute-start(bf16[4,4,2304]{2,1,0:T(4,128)(2,1)S(1)} %slice.42), channel_id=1, source_target_pairs={{0,4},{1,3},{2,6},{3,1},{4,0},{5,7},{6,2},{7,5},{8,12},{9,11},{10,... | collective-permute-start | bytes 221192 | tf_op jit(solution)/shard_map/ppermute | solution.py:35
  41.2 2.8 %collective-permute-done.6 = bf16[4,4,2304]{2,1,0:T(4,128)(2,1)S(1)} collective-permute-done((bf16[4,4,2304]{2,1,0:T(4,128)(2,1)S(1)}, bf16[4,4,2304]{2,1,0:T(4,128)(2,1)S(1)}, u32[]{:S(2)}, u32[]{:S(2)}) %collective-permute-start.6) | collective-permute-done | bytes 73760 | tf_op jit(solution)/shard_map/ppermute | solution.py:35
  44.2 2.7 %collective-permute-start.7 = (f32[4,2,2304]{2,1,0:T(2,128)S(1)}, f32[4,2,2304]{2,1,0:T(2,128)S(1)}, u32[]{:S(2)}, u32[]{:S(2)}) collective-permute-start(f32[4,2,2304]{2,1,0:T(2,128)S(1)} %slice.31), channel_id=1, source_target_pairs={{0,8},{1,9},{2,10},{3,11},{4,12},{5,13},{6,14},{7,15},{8,0},{9,1},... | collective-permute-start | bytes 221192 | tf_op jit(solution)/shard_map/ppermute | solution.py:35
  46.9 2.6 %collective-permute-done.7 = f32[4,2,2304]{2,1,0:T(2,128)S(1)} collective-permute-done((f32[4,2,2304]{2,1,0:T(2,128)S(1)}, f32[4,2,2304]{2,1,0:T(2,128)S(1)}, u32[]{:S(2)}, u32[]{:S(2)}) %collective-permute-start.7) | collective-permute-done | bytes 73760 | tf_op jit(solution)/shard_map/ppermute | solution.py:35
  49.5 0.7 %copy.7 = f32[2,4,2304]{2,1,0:T(4,128)} copy(f32[2,4,2304]{2,0,1:T(2,128)S(1)} %fusion.1) | data formatting | bytes 147456 | tf_op jit(solution)/shard_map/add | solution.py:212
  (20 shorter events, 0.3 us)
Async XLA Ops:
  0.0 6.6 %collective-permute-start = (bf16[2,4,2304]{2,1,0:T(4,128)(2,1)}, bf16[2,4,2304]{2,1,0:T(4,128)(2,1)S(1)}, u32[]{:S(2)}, u32[]{:S(2)}) collective-permute-start(bf16[2,4,2304]{2,1,0:T(4,128)(2,1)} %refs_1_.3), channel_id=1, source_target_pairs={{0,8},{1,9},{2,10},{3,11},{4,12},{5,13},{6,14},{7,15},{8,0},{9,1},... | collective-permute-start | bytes 110600 | tf_op jit(solution)/shard_map/ppermute | solution.py:35
  6.6 11.7 %slice-start = ((s8[18874368]{0:T(1024)(128)(4,1)}), s8[4194304]{0:T(1024)(128)(4,1)S(1)}, s32[]{:S(2)}) async-start(s8[18874368]{0:T(1024)(128)(4,1)} %bitcast.2), calls=%async_computation | async-start | bytes 8388608
  6.7 11.5 %slice-start.1 = ((s8[18874368]{0:T(1024)(128)(4,1)}), s8[4194304]{0:T(1024)(128)(4,1)S(1)}, s32[]{:S(2)}) async-start(s8[18874368]{0:T(1024)(128)(4,1)} %bitcast.2), calls=%async_computation.1 | async-start | bytes 8388608
  6.7 11.5 %slice-start.2 = ((s8[18874368]{0:T(1024)(128)(4,1)}), s8[4194304]{0:T(1024)(128)(4,1)S(1)}, s32[]{:S(2)}) async-start(s8[18874368]{0:T(1024)(128)(4,1)} %bitcast.2), calls=%async_computation.2 | async-start | bytes 8388608
  6.7 11.5 %slice-start.3 = ((s8[18874368]{0:T(1024)(128)(4,1)}), s8[4194304]{0:T(1024)(128)(4,1)S(1)}, s32[]{:S(2)}) async-start(s8[18874368]{0:T(1024)(128)(4,1)} %bitcast.2), calls=%async_computation.3 | async-start | bytes 8388608
  6.7 11.5 %slice-start.4 = ((s8[18874368]{0:T(1024)(128)(4,1)}), s8[2097152]{0:T(1024)(128)(4,1)S(1)}, s32[]{:S(2)}) async-start(s8[18874368]{0:T(1024)(128)(4,1)} %bitcast.2), calls=%async_computation.4 | async-start | bytes 4194304
  6.8 4.4 %collective-permute-start.1 = (bf16[4,4,2304]{2,1,0:T(4,128)(2,1)S(1)}, bf16[4,4,2304]{2,1,0:T(4,128)(2,1)S(1)}, u32[]{:S(2)}, u32[]{:S(2)}) collective-permute-start(bf16[4,4,2304]{2,1,0:T(4,128)(2,1)S(1)} %join.1.refs_0_), channel_id=1, source_target_pairs={{0,4},{1,3},{2,6},{3,1},{4,0},{5,7},{6,2},{7,5},{8,12},{9,11},{10,... | collective-permute-start | bytes 221192 | tf_op jit(solution)/shard_map/ppermute | solution.py:35
  11.2 5.2 %collective-permute-start.2 = (bf16[4,8,2304]{2,1,0:T(8,128)(2,1)S(1)}, bf16[4,8,2304]{2,1,0:T(8,128)(2,1)S(1)}, u32[]{:S(2)}, u32[]{:S(2)}) collective-permute-start(bf16[4,8,2304]{2,1,0:T(8,128)(2,1)S(1)} %pad_maximum_fusion.1.refs_0_), channel_id=1, source_target_pairs={{0,2},{1,5},{2,0},{3,7},{4,6},{5,1},{6,4},{7,3},{8,10},{9,13},{10,... | collective-permute-start | bytes 442376 | tf_op jit(solution)/shard_map/ppermute | solution.py:35
  16.6 1.6 %collective-permute-start.3 = (bf16[4,16,2304]{2,1,0:T(8,128)(2,1)S(1)}, bf16[4,16,2304]{2,1,0:T(8,128)(2,1)S(1)}, u32[]{:S(2)}, u32[]{:S(2)}) collective-permute-start(bf16[4,16,2304]{2,1,0:T(8,128)(2,1)S(1)} %pad_maximum_fusion.near), channel_id=1, source_target_pairs={{0,1},{1,0},{2,3},{3,2},{4,5},{5,4},{6,7},{7,6},{8,9},{9,8},{10,11... | collective-permute-start | bytes 884744 | tf_op jit(solution)/shard_map/ppermute | solution.py:35
  17.3 32.2 %copy-start = (f32[4,2304]{1,0:T(4,128)S(1)}, f32[4,2304]{1,0:T(4,128)}, u32[]{:S(2)}) copy-start(f32[4,2304]{1,0:T(4,128)} %param.10) | copy-start | bytes 110596
  32.2 2.1 %collective-permute-start.4 = (f32[4,16,2304]{2,1,0:T(8,128)S(1)}, f32[4,16,2304]{2,1,0:T(8,128)S(1)}, u32[]{:S(2)}, u32[]{:S(2)}) collective-permute-start(f32[4,16,2304]{2,1,0:T(8,128)S(1)} %get-tuple-element.26), channel_id=1, source_target_pairs={{0,1},{1,0},{2,3},{3,2},{4,5},{5,4},{6,7},{7,6},{8,9},{9,8},{10,11... | collective-permute-start | bytes 1769480 | tf_op jit(solution)/shard_map/ppermute | solution.py:35
  34.4 5.2 %collective-permute-start.5 = (bf16[4,8,2304]{2,1,0:T(8,128)(2,1)S(1)}, bf16[4,8,2304]{2,1,0:T(8,128)(2,1)S(1)}, u32[]{:S(2)}, u32[]{:S(2)}) collective-permute-start(bf16[4,8,2304]{2,1,0:T(8,128)(2,1)S(1)} %slice.41), channel_id=1, source_target_pairs={{0,2},{1,5},{2,0},{3,7},{4,6},{5,1},{6,4},{7,3},{8,10},{9,13},{10,... | collective-permute-start | bytes 442376 | tf_op jit(solution)/shard_map/ppermute | solution.py:35
  39.6 4.4 %collective-permute-start.6 = (bf16[4,4,2304]{2,1,0:T(4,128)(2,1)S(1)}, bf16[4,4,2304]{2,1,0:T(4,128)(2,1)S(1)}, u32[]{:S(2)}, u32[]{:S(2)}) collective-permute-start(bf16[4,4,2304]{2,1,0:T(4,128)(2,1)S(1)} %slice.42), channel_id=1, source_target_pairs={{0,4},{1,3},{2,6},{3,1},{4,0},{5,7},{6,2},{7,5},{8,12},{9,11},{10,... | collective-permute-start | bytes 221192 | tf_op jit(solution)/shard_map/ppermute | solution.py:35
  44.2 5.3 %collective-permute-start.7 = (f32[4,2,2304]{2,1,0:T(2,128)S(1)}, f32[4,2,2304]{2,1,0:T(2,128)S(1)}, u32[]{:S(2)}, u32[]{:S(2)}) collective-permute-start(f32[4,2,2304]{2,1,0:T(2,128)S(1)} %slice.31), channel_id=1, source_target_pairs={{0,8},{1,9},{2,10},{3,11},{4,12},{5,13},{6,14},{7,15},{8,0},{9,1},... | collective-permute-start | bytes 221192 | tf_op jit(solution)/shard_map/ppermute | solution.py:35

commit v6 on v5

--- a/solution.py
+++ b/solution.py
@@ -189,6 +189,7 @@
     held = layer_inputs
     for i, masks in enumerate(steps):
         came = swap(held, masks, size)
+        first = swap(held, (1, 1), size) if i == len(steps) - 1 else None
         parts = [(held, None)] if i == 0 else []
         hidden = 2 * features * width
         if i < len(early):
@@ -202,7 +203,7 @@
         if i == len(steps) - 1:
             enc_bias = got.pop()
         fetched += got
-    far = swap(held, (1, 1), size)
+    far = jnp.concatenate([first, swap(came, (1, 1), size)], axis=1)
     total, sent = transcode(steps, order, [step for step, _ in early], valid_count, held, far, enc_bias, encoder, decoder, fetched)
     total = total + swap(sent, (1, 1), size)
     for i, masks in reversed(list(enumerate(steps))):

time: 50.4 us -> 50.1 us (level)
    ppermute x8 -> x9, waiting for transfers between devices: 14.7 us -> 14.3 us  [swap(): lax.ppermute(value, 'pair', [(i, i ^ masks[i % 2]) for i in range(size)])]
    ppermute x8 -> x9, starting transfers between devices: 13.7 us -> 13.7 us  [swap(): lax.ppermute(value, 'pair', [(i, i ^ masks[i % 2]) for i in range(size)])]
  transfers between devices with their start and end apart: 8 -> 9, of which waited for: 8 -> 8; matrix products, arithmetic and copies ran while one was open for 0% -> 0% of each run, Pallas kernels for 11% -> 11%
where the time goes in v6:
time: 50.1 us; the launch traced here: 49.8 us
  Pallas kernels  19.8 us (40%)
  waiting for transfers between devices  14.3 us (29%)
  starting transfers between devices  13.7 us (27%)
  between operations  0.84 us (2%)
  local copies, waits for them, and re-layouts  0.78 us (2%)
    ppermute x9, waiting for transfers between devices, swap(): lax.ppermute(value, 'pair', [(i, i ^ masks[i % 2]) for i in range(size)])  14.3 us
    pallas_call x1, Pallas kernels, transcode(): pl.pallas_call(functools.partial(transcode_kernel, steps, order, ready),...  13.9 us
    ppermute x9, starting transfers between devices, swap(): lax.ppermute(value, 'pair', [(i, i ^ masks[i % 2]) for i in range(size)])  13.7 us
    pallas_call x3, Pallas kernels, fetch(): pl.pallas_call(functools.partial(fetch_kernel, [part[1] for part in parts...  5.71 us
  transfers between devices with their start and end apart: 9, of which 8 were waited for; matrix products, arithmetic and copies ran while one was open for 0% of the time, Pallas kernels for 11%

profile of v6, /device:TPU:0, one launch (start us, length us, event | category | flops | bytes accessed | tf_op | source)
XLA Modules:
  0.0 49.8 jit_solution(818324133356603095)
XLA Ops:
  0.0 4.0 %collective-permute-start = (bf16[2,4,2304]{2,1,0:T(4,128)(2,1)}, bf16[2,4,2304]{2,1,0:T(4,128)(2,1)S(1)}, u32[]{:S(2)}, u32[]{:S(2)}) collective-permute-start(bf16[2,4,2304]{2,1,0:T(4,128)(2,1)} %refs_1_.3), channel_id=1, source_target_pairs={{0,8},{1,9},{2,10},{3,11},{4,12},{5,13},{6,14},{7,15},{8,0},{9,1},... | collective-permute-start | bytes 110600 | tf_op jit(solution)/shard_map/ppermute | solution.py:35
  4.0 2.4 %fetch.3 = (bf16[2,4,2304]{2,1,0:T(4,128)(2,1)S(1)}, bf16[1024,2304]{1,0:T(8,128)(2,1)S(1)}) custom-call(bf16[2,4,2304]{2,1,0:T(4,128)(2,1)} %refs_1_.3, bf16[2,4,2304]{2,1,0:T(4,128)(2,1)} %refs_1_.3, bf16[10,1024,2304]{2,1,0:T(8,128)(2,1)} %decoder.1), custom_call_target="tpu_custom_call" | custom-call | bytes 4718592 | tf_op jit(solution)/shard_map/fetch/pallas_call | solution.py:56
  6.4 0.2 collective-permute-done.second
  6.6 0.1 join.1.refs_0_
  6.8 1.6 %collective-permute-start.1 = (bf16[4,4,2304]{2,1,0:T(4,128)(2,1)S(1)}, bf16[4,4,2304]{2,1,0:T(4,128)(2,1)S(1)}, u32[]{:S(2)}, u32[]{:S(2)}) collective-permute-start(bf16[4,4,2304]{2,1,0:T(4,128)(2,1)S(1)} %join.1.refs_0_), channel_id=1, source_target_pairs={{0,4},{1,3},{2,6},{3,1},{4,0},{5,7},{6,2},{7,5},{8,12},{9,11},{10,... | collective-permute-start | bytes 221192 | tf_op jit(solution)/shard_map/ppermute | solution.py:35
  8.3 2.6 %fetch.4.rest_1_ = bf16[640,2304]{1,0:T(8,128)(2,1)S(1)} custom-call(bf16[4,4,2304]{2,1,0:T(4,128)(2,1)S(1)} %join.1.refs_0_, bf16[10,1024,2304]{2,1,0:T(8,128)(2,1)} %decoder.1), custom_call_target="tpu_custom_call" | custom-call | bytes 4718592 | tf_op jit(solution)/shard_map/fetch/pallas_call | solution.py:56
  10.9 0.2 collective-permute-done.1
  11.2 0.1 pad_maximum_fusion.2.refs_0_
  11.2 1.8 %collective-permute-start.2 = (bf16[4,8,2304]{2,1,0:T(8,128)(2,1)S(1)}, bf16[4,8,2304]{2,1,0:T(8,128)(2,1)S(1)}, u32[]{:S(2)}, u32[]{:S(2)}) collective-permute-start(bf16[4,8,2304]{2,1,0:T(8,128)(2,1)S(1)} %pad_maximum_fusion.2.refs_0_), channel_id=1, source_target_pairs={{0,2},{1,5},{2,0},{3,7},{4,6},{5,1},{6,4},{7,3},{8,10},{9,13},{10,... | collective-permute-start | bytes 442376 | tf_op jit(solution)/shard_map/ppermute | solution.py:35
  13.7 0.1 collective-permute-start.3
  13.7 0.7 %fetch.5.bias = f32[4,1024]{1,0:T(4,128)S(1)} custom-call(bf16[4,8,2304]{2,1,0:T(8,128)(2,1)S(1)} %pad_maximum_fusion.2.refs_0_, f32[4,1024]{1,0:T(4,128)} %refs_1_.5), custom_call_target="tpu_custom_call" | custom-call | bytes 37748736 | tf_op jit(solution)/shard_map/fetch/pallas_call | solution.py:56
  14.5 2.0 %collective-permute-done.2 = bf16[4,8,2304]{2,1,0:T(8,128)(2,1)S(1)} collective-permute-done((bf16[4,8,2304]{2,1,0:T(8,128)(2,1)S(1)}, bf16[4,8,2304]{2,1,0:T(8,128)(2,1)S(1)}, u32[]{:S(2)}, u32[]{:S(2)}) %collective-permute-start.2) | collective-permute-done | bytes 147488 | tf_op jit(solution)/shard_map/ppermute | solution.py:35
  16.5 0.1 pad_maximum_fusion.near
  16.6 1.2 %collective-permute-done.4 = bf16[4,8,2304]{2,1,0:T(8,128)(2,1)S(1)} collective-permute-done((bf16[4,8,2304]{2,1,0:T(8,128)(2,1)S(1)}, bf16[4,8,2304]{2,1,0:T(8,128)(2,1)S(1)}, u32[]{:S(2)}, u32[]{:S(2)}) %collective-permute-start.4) | collective-permute-done | bytes 147488 | tf_op jit(solution)/shard_map/ppermute | solution.py:35
  17.9 13.9 %transcode.1 = (f32[4,16,2304]{2,1,0:T(8,128)S(1)}, f32[4,16,2304]{2,1,0:T(8,128)S(1)}) custom-call(s32[1]{0:T(128)S(6)} %copy.8.limit, bf16[4,16,2304]{2,1,0:T(8,128)(2,1)S(1)} %pad_maximum_fusion.near, bf16[4,16,2304]{2,1,0:T(8,128)(2,1)S(1)} %pad_maximum_fusion.1.far, f32[4,1024]{1,0:T(4,128)S(1)} %fetch.5.bias, bf16[4,2304,1024]{2,1,0:T(8,128)(2,1)S(1)} %bitcast.3, ...), custom_call_target="tpu_custom_call" | custom-call | tf_op jit(solution)/shard_map/transcode/pallas_call | solution.py:168
  31.9 0.2 collective-permute-start.5
  32.1 1.9 %collective-permute-done.5 = f32[4,16,2304]{2,1,0:T(8,128)S(1)} collective-permute-done((f32[4,16,2304]{2,1,0:T(8,128)S(1)}, f32[4,16,2304]{2,1,0:T(8,128)S(1)}, u32[]{:S(2)}, u32[]{:S(2)}) %collective-permute-start.5) | collective-permute-done | bytes 589856 | tf_op jit(solution)/shard_map/ppermute | solution.py:35
  34.0 1.8 %collective-permute-start.6 = (bf16[4,8,2304]{2,1,0:T(8,128)(2,1)S(1)}, bf16[4,8,2304]{2,1,0:T(8,128)(2,1)S(1)}, u32[]{:S(2)}, u32[]{:S(2)}) collective-permute-start(bf16[4,8,2304]{2,1,0:T(8,128)(2,1)S(1)} %slice.41), channel_id=1, source_target_pairs={{0,2},{1,5},{2,0},{3,7},{4,6},{5,1},{6,4},{7,3},{8,10},{9,13},{10,... | collective-permute-start | bytes 442376 | tf_op jit(solution)/shard_map/ppermute | solution.py:35
  35.8 3.4 %collective-permute-done.6 = bf16[4,8,2304]{2,1,0:T(8,128)(2,1)S(1)} collective-permute-done((bf16[4,8,2304]{2,1,0:T(8,128)(2,1)S(1)}, bf16[4,8,2304]{2,1,0:T(8,128)(2,1)S(1)}, u32[]{:S(2)}, u32[]{:S(2)}) %collective-permute-start.6) | collective-permute-done | bytes 147488 | tf_op jit(solution)/shard_map/ppermute | solution.py:35
  39.3 1.6 %collective-permute-start.7 = (bf16[4,4,2304]{2,1,0:T(4,128)(2,1)S(1)}, bf16[4,4,2304]{2,1,0:T(4,128)(2,1)S(1)}, u32[]{:S(2)}, u32[]{:S(2)}) collective-permute-start(bf16[4,4,2304]{2,1,0:T(4,128)(2,1)S(1)} %slice.42), channel_id=1, source_target_pairs={{0,4},{1,3},{2,6},{3,1},{4,0},{5,7},{6,2},{7,5},{8,12},{9,11},{10,... | collective-permute-start | bytes 221192 | tf_op jit(solution)/shard_map/ppermute | solution.py:35
  40.9 2.8 %collective-permute-done.7 = bf16[4,4,2304]{2,1,0:T(4,128)(2,1)S(1)} collective-permute-done((bf16[4,4,2304]{2,1,0:T(4,128)(2,1)S(1)}, bf16[4,4,2304]{2,1,0:T(4,128)(2,1)S(1)}, u32[]{:S(2)}, u32[]{:S(2)}) %collective-permute-start.7) | collective-permute-done | bytes 73760 | tf_op jit(solution)/shard_map/ppermute | solution.py:35
  43.8 2.7 %collective-permute-start.8 = (f32[4,2,2304]{2,1,0:T(2,128)S(1)}, f32[4,2,2304]{2,1,0:T(2,128)S(1)}, u32[]{:S(2)}, u32[]{:S(2)}) collective-permute-start(f32[4,2,2304]{2,1,0:T(2,128)S(1)} %slice.31), channel_id=1, source_target_pairs={{0,8},{1,9},{2,10},{3,11},{4,12},{5,13},{6,14},{7,15},{8,0},{9,1},... | collective-permute-start | bytes 221192 | tf_op jit(solution)/shard_map/ppermute | solution.py:35
  46.5 2.6 %collective-permute-done.8 = f32[4,2,2304]{2,1,0:T(2,128)S(1)} collective-permute-done((f32[4,2,2304]{2,1,0:T(2,128)S(1)}, f32[4,2,2304]{2,1,0:T(2,128)S(1)}, u32[]{:S(2)}, u32[]{:S(2)}) %collective-permute-start.8) | collective-permute-done | bytes 73760 | tf_op jit(solution)/shard_map/ppermute | solution.py:35
  49.2 0.7 %copy.7 = f32[2,4,2304]{2,1,0:T(4,128)} copy(f32[2,4,2304]{2,0,1:T(2,128)S(1)} %fusion.1) | data formatting | bytes 147456 | tf_op jit(solution)/shard_map/add | solution.py:213
  (23 shorter events, 0.3 us)
Async XLA Ops:
  0.0 6.6 %collective-permute-start = (bf16[2,4,2304]{2,1,0:T(4,128)(2,1)}, bf16[2,4,2304]{2,1,0:T(4,128)(2,1)S(1)}, u32[]{:S(2)}, u32[]{:S(2)}) collective-permute-start(bf16[2,4,2304]{2,1,0:T(4,128)(2,1)} %refs_1_.3), channel_id=1, source_target_pairs={{0,8},{1,9},{2,10},{3,11},{4,12},{5,13},{6,14},{7,15},{8,0},{9,1},... | collective-permute-start | bytes 110600 | tf_op jit(solution)/shard_map/ppermute | solution.py:35
  6.6 11.3 %slice-start = ((s8[18874368]{0:T(1024)(128)(4,1)}), s8[4194304]{0:T(1024)(128)(4,1)S(1)}, s32[]{:S(2)}) async-start(s8[18874368]{0:T(1024)(128)(4,1)} %bitcast.2), calls=%async_computation | async-start | bytes 8388608
  6.7 11.2 %slice-start.1 = ((s8[18874368]{0:T(1024)(128)(4,1)}), s8[4194304]{0:T(1024)(128)(4,1)S(1)}, s32[]{:S(2)}) async-start(s8[18874368]{0:T(1024)(128)(4,1)} %bitcast.2), calls=%async_computation.1 | async-start | bytes 8388608
  6.7 11.2 %slice-start.2 = ((s8[18874368]{0:T(1024)(128)(4,1)}), s8[4194304]{0:T(1024)(128)(4,1)S(1)}, s32[]{:S(2)}) async-start(s8[18874368]{0:T(1024)(128)(4,1)} %bitcast.2), calls=%async_computation.2 | async-start | bytes 8388608
  6.7 11.2 %slice-start.3 = ((s8[18874368]{0:T(1024)(128)(4,1)}), s8[4194304]{0:T(1024)(128)(4,1)S(1)}, s32[]{:S(2)}) async-start(s8[18874368]{0:T(1024)(128)(4,1)} %bitcast.2), calls=%async_computation.3 | async-start | bytes 8388608
  6.7 11.2 %slice-start.4 = ((s8[18874368]{0:T(1024)(128)(4,1)}), s8[2097152]{0:T(1024)(128)(4,1)S(1)}, s32[]{:S(2)}) async-start(s8[18874368]{0:T(1024)(128)(4,1)} %bitcast.2), calls=%async_computation.4 | async-start | bytes 4194304
  6.8 4.4 %collective-permute-start.1 = (bf16[4,4,2304]{2,1,0:T(4,128)(2,1)S(1)}, bf16[4,4,2304]{2,1,0:T(4,128)(2,1)S(1)}, u32[]{:S(2)}, u32[]{:S(2)}) collective-permute-start(bf16[4,4,2304]{2,1,0:T(4,128)(2,1)S(1)} %join.1.refs_0_), channel_id=1, source_target_pairs={{0,4},{1,3},{2,6},{3,1},{4,0},{5,7},{6,2},{7,5},{8,12},{9,11},{10,... | collective-permute-start | bytes 221192 | tf_op jit(solution)/shard_map/ppermute | solution.py:35
  11.2 5.2 %collective-permute-start.2 = (bf16[4,8,2304]{2,1,0:T(8,128)(2,1)S(1)}, bf16[4,8,2304]{2,1,0:T(8,128)(2,1)S(1)}, u32[]{:S(2)}, u32[]{:S(2)}) collective-permute-start(bf16[4,8,2304]{2,1,0:T(8,128)(2,1)S(1)} %pad_maximum_fusion.2.refs_0_), channel_id=1, source_target_pairs={{0,2},{1,5},{2,0},{3,7},{4,6},{5,1},{6,4},{7,3},{8,10},{9,13},{10,... | collective-permute-start | bytes 442376 | tf_op jit(solution)/shard_map/ppermute | solution.py:35
  13.7 2.9 %collective-permute-start.3 = (bf16[4,8,2304]{2,1,0:T(8,128)(2,1)S(1)}, bf16[4,8,2304]{2,1,0:T(8,128)(2,1)S(1)}, u32[]{:S(2)}, u32[]{:S(2)}) collective-permute-start(bf16[4,8,2304]{2,1,0:T(8,128)(2,1)S(1)} %pad_maximum_fusion.2.refs_0_), channel_id=1, source_target_pairs={{0,1},{1,0},{2,3},{3,2},{4,5},{5,4},{6,7},{7,6},{8,9},{9,8},{10,11... | collective-permute-start | bytes 442376 | tf_op jit(solution)/shard_map/ppermute | solution.py:35
  16.5 1.4 %collective-permute-start.4 = (bf16[4,8,2304]{2,1,0:T(8,128)(2,1)S(1)}, bf16[4,8,2304]{2,1,0:T(8,128)(2,1)S(1)}, u32[]{:S(2)}, u32[]{:S(2)}) collective-permute-start(bf16[4,8,2304]{2,1,0:T(8,128)(2,1)S(1)} %collective-permute-done.2), channel_id=1, source_target_pairs={{0,1},{1,0},{2,3},{3,2},{4,5},{5,4},{6,7},{7,6},{8,9},{9,8},{10,11... | collective-permute-start | bytes 442376 | tf_op jit(solution)/shard_map/ppermute | solution.py:35
  17.9 31.2 %copy-start = (f32[4,2304]{1,0:T(4,128)S(1)}, f32[4,2304]{1,0:T(4,128)}, u32[]{:S(2)}) copy-start(f32[4,2304]{1,0:T(4,128)} %param.10) | copy-start | bytes 110596
  31.9 2.1 %collective-permute-start.5 = (f32[4,16,2304]{2,1,0:T(8,128)S(1)}, f32[4,16,2304]{2,1,0:T(8,128)S(1)}, u32[]{:S(2)}, u32[]{:S(2)}) collective-permute-start(f32[4,16,2304]{2,1,0:T(8,128)S(1)} %get-tuple-element.26), channel_id=1, source_target_pairs={{0,1},{1,0},{2,3},{3,2},{4,5},{5,4},{6,7},{7,6},{8,9},{9,8},{10,11... | collective-permute-start | bytes 1769480 | tf_op jit(solution)/shard_map/ppermute | solution.py:35
  34.0 5.2 %collective-permute-start.6 = (bf16[4,8,2304]{2,1,0:T(8,128)(2,1)S(1)}, bf16[4,8,2304]{2,1,0:T(8,128)(2,1)S(1)}, u32[]{:S(2)}, u32[]{:S(2)}) collective-permute-start(bf16[4,8,2304]{2,1,0:T(8,128)(2,1)S(1)} %slice.41), channel_id=1, source_target_pairs={{0,2},{1,5},{2,0},{3,7},{4,6},{5,1},{6,4},{7,3},{8,10},{9,13},{10,... | collective-permute-start | bytes 442376 | tf_op jit(solution)/shard_map/ppermute | solution.py:35
  39.3 4.4 %collective-permute-start.7 = (bf16[4,4,2304]{2,1,0:T(4,128)(2,1)S(1)}, bf16[4,4,2304]{2,1,0:T(4,128)(2,1)S(1)}, u32[]{:S(2)}, u32[]{:S(2)}) collective-permute-start(bf16[4,4,2304]{2,1,0:T(4,128)(2,1)S(1)} %slice.42), channel_id=1, source_target_pairs={{0,4},{1,3},{2,6},{3,1},{4,0},{5,7},{6,2},{7,5},{8,12},{9,11},{10,... | collective-permute-start | bytes 221192 | tf_op jit(solution)/shard_map/ppermute | solution.py:35
  43.8 5.3 %collective-permute-start.8 = (f32[4,2,2304]{2,1,0:T(2,128)S(1)}, f32[4,2,2304]{2,1,0:T(2,128)S(1)}, u32[]{:S(2)}, u32[]{:S(2)}) collective-permute-start(f32[4,2,2304]{2,1,0:T(2,128)S(1)} %slice.31), channel_id=1, source_target_pairs={{0,8},{1,9},{2,10},{3,11},{4,12},{5,13},{6,14},{7,15},{8,0},{9,1},... | collective-permute-start | bytes 221192 | tf_op jit(solution)/shard_map/ppermute | solution.py:35

commit v7 on v6

--- a/solution.py
+++ b/solution.py
@@ -12,7 +12,7 @@
 SMEM = pl.BlockSpec(memory_space=pltpu.SMEM)
 ANY = pl.BlockSpec(memory_space=pl.ANY)
 SLOTS = 4
-CHUNK = 768
+CHUNK = 512
 
 
 def pair_index(source, target, layers):

time: 50.1 us -> 50.1 us (level)
  no operation moved by 1% of the time
where the time goes in v7:
time: 50.1 us; the launch traced here: 49.8 us
  Pallas kernels  19.8 us (40%)
  waiting for transfers between devices  14.3 us (29%)
  starting transfers between devices  13.7 us (27%)
  between operations  0.84 us (2%)
  local copies, waits for them, and re-layouts  0.78 us (2%)
    ppermute x9, waiting for transfers between devices, swap(): lax.ppermute(value, 'pair', [(i, i ^ masks[i % 2]) for i in range(size)])  14.3 us
    pallas_call x1, Pallas kernels, transcode(): pl.pallas_call(functools.partial(transcode_kernel, steps, order, ready),...  13.9 us
    ppermute x9, starting transfers between devices, swap(): lax.ppermute(value, 'pair', [(i, i ^ masks[i % 2]) for i in range(size)])  13.7 us
    pallas_call x3, Pallas kernels, fetch(): pl.pallas_call(functools.partial(fetch_kernel, [part[1] for part in parts...  5.71 us
  transfers between devices with their start and end apart: 9, of which 8 were waited for; matrix products, arithmetic and copies ran while one was open for 0% of the time, Pallas kernels for 11%

profile of v7, /device:TPU:0, one launch (start us, length us, event | category | flops | bytes accessed | tf_op | source)
XLA Modules:
  0.0 49.8 jit_solution(818324133356603095)
XLA Ops:
  0.0 4.0 %collective-permute-start = (bf16[2,4,2304]{2,1,0:T(4,128)(2,1)}, bf16[2,4,2304]{2,1,0:T(4,128)(2,1)S(1)}, u32[]{:S(2)}, u32[]{:S(2)}) collective-permute-start(bf16[2,4,2304]{2,1,0:T(4,128)(2,1)} %refs_1_.3), channel_id=1, source_target_pairs={{0,8},{1,9},{2,10},{3,11},{4,12},{5,13},{6,14},{7,15},{8,0},{9,1},... | collective-permute-start | bytes 110600 | tf_op jit(solution)/shard_map/ppermute | solution.py:35
  4.0 2.4 %fetch.3 = (bf16[2,4,2304]{2,1,0:T(4,128)(2,1)S(1)}, bf16[1024,2304]{1,0:T(8,128)(2,1)S(1)}) custom-call(bf16[2,4,2304]{2,1,0:T(4,128)(2,1)} %refs_1_.3, bf16[2,4,2304]{2,1,0:T(4,128)(2,1)} %refs_1_.3, bf16[10,1024,2304]{2,1,0:T(8,128)(2,1)} %decoder.1), custom_call_target="tpu_custom_call" | custom-call | bytes 4718592 | tf_op jit(solution)/shard_map/fetch/pallas_call | solution.py:56
  6.4 0.2 collective-permute-done.second
  6.6 0.1 join.1.refs_0_
  6.8 1.6 %collective-permute-start.1 = (bf16[4,4,2304]{2,1,0:T(4,128)(2,1)S(1)}, bf16[4,4,2304]{2,1,0:T(4,128)(2,1)S(1)}, u32[]{:S(2)}, u32[]{:S(2)}) collective-permute-start(bf16[4,4,2304]{2,1,0:T(4,128)(2,1)S(1)} %join.1.refs_0_), channel_id=1, source_target_pairs={{0,4},{1,3},{2,6},{3,1},{4,0},{5,7},{6,2},{7,5},{8,12},{9,11},{10,... | collective-permute-start | bytes 221192 | tf_op jit(solution)/shard_map/ppermute | solution.py:35
  8.3 2.6 %fetch.4.rest_1_ = bf16[640,2304]{1,0:T(8,128)(2,1)S(1)} custom-call(bf16[4,4,2304]{2,1,0:T(4,128)(2,1)S(1)} %join.1.refs_0_, bf16[10,1024,2304]{2,1,0:T(8,128)(2,1)} %decoder.1), custom_call_target="tpu_custom_call" | custom-call | bytes 4718592 | tf_op jit(solution)/shard_map/fetch/pallas_call | solution.py:56
  10.9 0.2 collective-permute-done.1
  11.2 0.1 pad_maximum_fusion.2.refs_0_
  11.2 1.8 %collective-permute-start.2 = (bf16[4,8,2304]{2,1,0:T(8,128)(2,1)S(1)}, bf16[4,8,2304]{2,1,0:T(8,128)(2,1)S(1)}, u32[]{:S(2)}, u32[]{:S(2)}) collective-permute-start(bf16[4,8,2304]{2,1,0:T(8,128)(2,1)S(1)} %pad_maximum_fusion.2.refs_0_), channel_id=1, source_target_pairs={{0,2},{1,5},{2,0},{3,7},{4,6},{5,1},{6,4},{7,3},{8,10},{9,13},{10,... | collective-permute-start | bytes 442376 | tf_op jit(solution)/shard_map/ppermute | solution.py:35
  13.7 0.1 collective-permute-start.3
  13.7 0.7 %fetch.5.bias = f32[4,1024]{1,0:T(4,128)S(1)} custom-call(bf16[4,8,2304]{2,1,0:T(8,128)(2,1)S(1)} %pad_maximum_fusion.2.refs_0_, f32[4,1024]{1,0:T(4,128)} %refs_1_.5), custom_call_target="tpu_custom_call" | custom-call | bytes 37748736 | tf_op jit(solution)/shard_map/fetch/pallas_call | solution.py:56
  14.5 2.0 %collective-permute-done.2 = bf16[4,8,2304]{2,1,0:T(8,128)(2,1)S(1)} collective-permute-done((bf16[4,8,2304]{2,1,0:T(8,128)(2,1)S(1)}, bf16[4,8,2304]{2,1,0:T(8,128)(2,1)S(1)}, u32[]{:S(2)}, u32[]{:S(2)}) %collective-permute-start.2) | collective-permute-done | bytes 147488 | tf_op jit(solution)/shard_map/ppermute | solution.py:35
  16.5 0.1 pad_maximum_fusion.near
  16.6 1.2 %collective-permute-done.4 = bf16[4,8,2304]{2,1,0:T(8,128)(2,1)S(1)} collective-permute-done((bf16[4,8,2304]{2,1,0:T(8,128)(2,1)S(1)}, bf16[4,8,2304]{2,1,0:T(8,128)(2,1)S(1)}, u32[]{:S(2)}, u32[]{:S(2)}) %collective-permute-start.4) | collective-permute-done | bytes 147488 | tf_op jit(solution)/shard_map/ppermute | solution.py:35
  17.9 13.9 %transcode.1 = (f32[4,16,2304]{2,1,0:T(8,128)S(1)}, f32[4,16,2304]{2,1,0:T(8,128)S(1)}) custom-call(s32[1]{0:T(128)S(6)} %copy.8.limit, bf16[4,16,2304]{2,1,0:T(8,128)(2,1)S(1)} %pad_maximum_fusion.near, bf16[4,16,2304]{2,1,0:T(8,128)(2,1)S(1)} %pad_maximum_fusion.1.far, f32[4,1024]{1,0:T(4,128)S(1)} %fetch.5.bias, bf16[4,2304,1024]{2,1,0:T(8,128)(2,1)S(1)} %bitcast.3, ...), custom_call_target="tpu_custom_call" | custom-call | tf_op jit(solution)/shard_map/transcode/pallas_call | solution.py:168
  31.9 0.2 collective-permute-start.5
  32.1 1.9 %collective-permute-done.5 = f32[4,16,2304]{2,1,0:T(8,128)S(1)} collective-permute-done((f32[4,16,2304]{2,1,0:T(8,128)S(1)}, f32[4,16,2304]{2,1,0:T(8,128)S(1)}, u32[]{:S(2)}, u32[]{:S(2)}) %collective-permute-start.5) | collective-permute-done | bytes 589856 | tf_op jit(solution)/shard_map/ppermute | solution.py:35
  34.0 1.8 %collective-permute-start.6 = (bf16[4,8,2304]{2,1,0:T(8,128)(2,1)S(1)}, bf16[4,8,2304]{2,1,0:T(8,128)(2,1)S(1)}, u32[]{:S(2)}, u32[]{:S(2)}) collective-permute-start(bf16[4,8,2304]{2,1,0:T(8,128)(2,1)S(1)} %slice.41), channel_id=1, source_target_pairs={{0,2},{1,5},{2,0},{3,7},{4,6},{5,1},{6,4},{7,3},{8,10},{9,13},{10,... | collective-permute-start | bytes 442376 | tf_op jit(solution)/shard_map/ppermute | solution.py:35
  35.8 3.4 %collective-permute-done.6 = bf16[4,8,2304]{2,1,0:T(8,128)(2,1)S(1)} collective-permute-done((bf16[4,8,2304]{2,1,0:T(8,128)(2,1)S(1)}, bf16[4,8,2304]{2,1,0:T(8,128)(2,1)S(1)}, u32[]{:S(2)}, u32[]{:S(2)}) %collective-permute-start.6) | collective-permute-done | bytes 147488 | tf_op jit(solution)/shard_map/ppermute | solution.py:35
  39.3 1.6 %collective-permute-start.7 = (bf16[4,4,2304]{2,1,0:T(4,128)(2,1)S(1)}, bf16[4,4,2304]{2,1,0:T(4,128)(2,1)S(1)}, u32[]{:S(2)}, u32[]{:S(2)}) collective-permute-start(bf16[4,4,2304]{2,1,0:T(4,128)(2,1)S(1)} %slice.42), channel_id=1, source_target_pairs={{0,4},{1,3},{2,6},{3,1},{4,0},{5,7},{6,2},{7,5},{8,12},{9,11},{10,... | collective-permute-start | bytes 221192 | tf_op jit(solution)/shard_map/ppermute | solution.py:35
  40.9 2.8 %collective-permute-done.7 = bf16[4,4,2304]{2,1,0:T(4,128)(2,1)S(1)} collective-permute-done((bf16[4,4,2304]{2,1,0:T(4,128)(2,1)S(1)}, bf16[4,4,2304]{2,1,0:T(4,128)(2,1)S(1)}, u32[]{:S(2)}, u32[]{:S(2)}) %collective-permute-start.7) | collective-permute-done | bytes 73760 | tf_op jit(solution)/shard_map/ppermute | solution.py:35
  43.8 2.7 %collective-permute-start.8 = (f32[4,2,2304]{2,1,0:T(2,128)S(1)}, f32[4,2,2304]{2,1,0:T(2,128)S(1)}, u32[]{:S(2)}, u32[]{:S(2)}) collective-permute-start(f32[4,2,2304]{2,1,0:T(2,128)S(1)} %slice.31), channel_id=1, source_target_pairs={{0,8},{1,9},{2,10},{3,11},{4,12},{5,13},{6,14},{7,15},{8,0},{9,1},... | collective-permute-start | bytes 221192 | tf_op jit(solution)/shard_map/ppermute | solution.py:35
  46.5 2.6 %collective-permute-done.8 = f32[4,2,2304]{2,1,0:T(2,128)S(1)} collective-permute-done((f32[4,2,2304]{2,1,0:T(2,128)S(1)}, f32[4,2,2304]{2,1,0:T(2,128)S(1)}, u32[]{:S(2)}, u32[]{:S(2)}) %collective-permute-start.8) | collective-permute-done | bytes 73760 | tf_op jit(solution)/shard_map/ppermute | solution.py:35
  49.2 0.7 %copy.7 = f32[2,4,2304]{2,1,0:T(4,128)} copy(f32[2,4,2304]{2,0,1:T(2,128)S(1)} %fusion.1) | data formatting | bytes 147456 | tf_op jit(solution)/shard_map/add | solution.py:213
  (23 shorter events, 0.3 us)
Async XLA Ops:
  0.0 6.6 %collective-permute-start = (bf16[2,4,2304]{2,1,0:T(4,128)(2,1)}, bf16[2,4,2304]{2,1,0:T(4,128)(2,1)S(1)}, u32[]{:S(2)}, u32[]{:S(2)}) collective-permute-start(bf16[2,4,2304]{2,1,0:T(4,128)(2,1)} %refs_1_.3), channel_id=1, source_target_pairs={{0,8},{1,9},{2,10},{3,11},{4,12},{5,13},{6,14},{7,15},{8,0},{9,1},... | collective-permute-start | bytes 110600 | tf_op jit(solution)/shard_map/ppermute | solution.py:35
  6.6 11.3 %slice-start = ((s8[18874368]{0:T(1024)(128)(4,1)}), s8[4194304]{0:T(1024)(128)(4,1)S(1)}, s32[]{:S(2)}) async-start(s8[18874368]{0:T(1024)(128)(4,1)} %bitcast.2), calls=%async_computation | async-start | bytes 8388608
  6.7 11.2 %slice-start.1 = ((s8[18874368]{0:T(1024)(128)(4,1)}), s8[4194304]{0:T(1024)(128)(4,1)S(1)}, s32[]{:S(2)}) async-start(s8[18874368]{0:T(1024)(128)(4,1)} %bitcast.2), calls=%async_computation.1 | async-start | bytes 8388608
  6.7 11.2 %slice-start.2 = ((s8[18874368]{0:T(1024)(128)(4,1)}), s8[4194304]{0:T(1024)(128)(4,1)S(1)}, s32[]{:S(2)}) async-start(s8[18874368]{0:T(1024)(128)(4,1)} %bitcast.2), calls=%async_computation.2 | async-start | bytes 8388608
  6.7 11.2 %slice-start.3 = ((s8[18874368]{0:T(1024)(128)(4,1)}), s8[4194304]{0:T(1024)(128)(4,1)S(1)}, s32[]{:S(2)}) async-start(s8[18874368]{0:T(1024)(128)(4,1)} %bitcast.2), calls=%async_computation.3 | async-start | bytes 8388608
  6.7 11.2 %slice-start.4 = ((s8[18874368]{0:T(1024)(128)(4,1)}), s8[2097152]{0:T(1024)(128)(4,1)S(1)}, s32[]{:S(2)}) async-start(s8[18874368]{0:T(1024)(128)(4,1)} %bitcast.2), calls=%async_computation.4 | async-start | bytes 4194304
  6.8 4.4 %collective-permute-start.1 = (bf16[4,4,2304]{2,1,0:T(4,128)(2,1)S(1)}, bf16[4,4,2304]{2,1,0:T(4,128)(2,1)S(1)}, u32[]{:S(2)}, u32[]{:S(2)}) collective-permute-start(bf16[4,4,2304]{2,1,0:T(4,128)(2,1)S(1)} %join.1.refs_0_), channel_id=1, source_target_pairs={{0,4},{1,3},{2,6},{3,1},{4,0},{5,7},{6,2},{7,5},{8,12},{9,11},{10,... | collective-permute-start | bytes 221192 | tf_op jit(solution)/shard_map/ppermute | solution.py:35
  11.2 5.2 %collective-permute-start.2 = (bf16[4,8,2304]{2,1,0:T(8,128)(2,1)S(1)}, bf16[4,8,2304]{2,1,0:T(8,128)(2,1)S(1)}, u32[]{:S(2)}, u32[]{:S(2)}) collective-permute-start(bf16[4,8,2304]{2,1,0:T(8,128)(2,1)S(1)} %pad_maximum_fusion.2.refs_0_), channel_id=1, source_target_pairs={{0,2},{1,5},{2,0},{3,7},{4,6},{5,1},{6,4},{7,3},{8,10},{9,13},{10,... | collective-permute-start | bytes 442376 | tf_op jit(solution)/shard_map/ppermute | solution.py:35
  13.7 2.9 %collective-permute-start.3 = (bf16[4,8,2304]{2,1,0:T(8,128)(2,1)S(1)}, bf16[4,8,2304]{2,1,0:T(8,128)(2,1)S(1)}, u32[]{:S(2)}, u32[]{:S(2)}) collective-permute-start(bf16[4,8,2304]{2,1,0:T(8,128)(2,1)S(1)} %pad_maximum_fusion.2.refs_0_), channel_id=1, source_target_pairs={{0,1},{1,0},{2,3},{3,2},{4,5},{5,4},{6,7},{7,6},{8,9},{9,8},{10,11... | collective-permute-start | bytes 442376 | tf_op jit(solution)/shard_map/ppermute | solution.py:35
  16.5 1.4 %collective-permute-start.4 = (bf16[4,8,2304]{2,1,0:T(8,128)(2,1)S(1)}, bf16[4,8,2304]{2,1,0:T(8,128)(2,1)S(1)}, u32[]{:S(2)}, u32[]{:S(2)}) collective-permute-start(bf16[4,8,2304]{2,1,0:T(8,128)(2,1)S(1)} %collective-permute-done.2), channel_id=1, source_target_pairs={{0,1},{1,0},{2,3},{3,2},{4,5},{5,4},{6,7},{7,6},{8,9},{9,8},{10,11... | collective-permute-start | bytes 442376 | tf_op jit(solution)/shard_map/ppermute | solution.py:35
  17.9 31.2 %copy-start = (f32[4,2304]{1,0:T(4,128)S(1)}, f32[4,2304]{1,0:T(4,128)}, u32[]{:S(2)}) copy-start(f32[4,2304]{1,0:T(4,128)} %param.10) | copy-start | bytes 110596
  31.9 2.1 %collective-permute-start.5 = (f32[4,16,2304]{2,1,0:T(8,128)S(1)}, f32[4,16,2304]{2,1,0:T(8,128)S(1)}, u32[]{:S(2)}, u32[]{:S(2)}) collective-permute-start(f32[4,16,2304]{2,1,0:T(8,128)S(1)} %get-tuple-element.26), channel_id=1, source_target_pairs={{0,1},{1,0},{2,3},{3,2},{4,5},{5,4},{6,7},{7,6},{8,9},{9,8},{10,11... | collective-permute-start | bytes 1769480 | tf_op jit(solution)/shard_map/ppermute | solution.py:35
  34.0 5.2 %collective-permute-start.6 = (bf16[4,8,2304]{2,1,0:T(8,128)(2,1)S(1)}, bf16[4,8,2304]{2,1,0:T(8,128)(2,1)S(1)}, u32[]{:S(2)}, u32[]{:S(2)}) collective-permute-start(bf16[4,8,2304]{2,1,0:T(8,128)(2,1)S(1)} %slice.41), channel_id=1, source_target_pairs={{0,2},{1,5},{2,0},{3,7},{4,6},{5,1},{6,4},{7,3},{8,10},{9,13},{10,... | collective-permute-start | bytes 442376 | tf_op jit(solution)/shard_map/ppermute | solution.py:35
  39.3 4.4 %collective-permute-start.7 = (bf16[4,4,2304]{2,1,0:T(4,128)(2,1)S(1)}, bf16[4,4,2304]{2,1,0:T(4,128)(2,1)S(1)}, u32[]{:S(2)}, u32[]{:S(2)}) collective-permute-start(bf16[4,4,2304]{2,1,0:T(4,128)(2,1)S(1)} %slice.42), channel_id=1, source_target_pairs={{0,4},{1,3},{2,6},{3,1},{4,0},{5,7},{6,2},{7,5},{8,12},{9,11},{10,... | collective-permute-start | bytes 221192 | tf_op jit(solution)/shard_map/ppermute | solution.py:35
  43.8 5.3 %collective-permute-start.8 = (f32[4,2,2304]{2,1,0:T(2,128)S(1)}, f32[4,2,2304]{2,1,0:T(2,128)S(1)}, u32[]{:S(2)}, u32[]{:S(2)}) collective-permute-start(f32[4,2,2304]{2,1,0:T(2,128)S(1)} %slice.31), channel_id=1, source_target_pairs={{0,8},{1,9},{2,10},{3,11},{4,12},{5,13},{6,14},{7,15},{8,0},{9,1},... | collective-permute-start | bytes 221192 | tf_op jit(solution)/shard_map/ppermute | solution.py:35
